TPU v7x, 32 devices: a whole 2x2x4 slice. The times are simulated.
32 devices in a mesh: dp: 8 (over y, x, core), tensor: 4 (over z).
Axes of the slice: x: 2, y: 2, z: 4, core: 2. Of those that a mesh axis runs over, the one named last changes fastest.
Arguments:
- inputs: bfloat16 [2048, 1792], P('dp', 'tensor'), may hold values from -6 to 6
- cotangent: bfloat16 [2048, 1792], P('dp', 'tensor'), may hold values from -6 to 6
- documents: int32 [2048], P('dp'), may hold values from -1 to 3, as said below
- gains: bfloat16 [2, 1792], P(None, 'tensor'), may hold values from 0.5 to 1.5
- query_key: bfloat16 [1792, 2, 256], P(None, None, 'tensor'), may hold values from -0.125 to 0.125
- value_gate: bfloat16 [1792, 2, 1792], P(None, None, 'tensor'), may hold values from -0.125 to 0.125
- conv_taps: bfloat16 [4, 1792], P(None, 'tensor'), may hold values from -3 to 3
- output_weight: bfloat16 [1792, 1792], P('tensor'), may hold values from -3 to 3
- gate_up: bfloat16 [1792, 2, 4096], P(None, None, 'tensor'), may hold values from -0.125 to 0.125
- down_weight: bfloat16 [4096, 1792], P('tensor'), may hold values from -0.09375 to 0.09375
- gains_moment: float32 [2, 1792], P(None, 'tensor'), may hold values from -60 to 60
- query_key_moment: float32 [1792, 2, 256], P('dp', None, 'tensor'), may hold values from -60 to 60
- value_gate_moment: float32 [1792, 2, 1792], P('dp', None, 'tensor'), may hold values from -60 to 60
- conv_taps_moment: float32 [4, 1792], P(None, 'tensor'), may hold values from -60 to 60
- output_weight_moment: float32 [1792, 1792], P('tensor', 'dp'), may hold values from -60 to 60
- gate_up_moment: float32 [1792, 2, 4096], P('dp', None, 'tensor'), may hold values from -60 to 60
- down_weight_moment: float32 [4096, 1792], P('tensor', 'dp'), may hold values from -60 to 60
- gains_mean: float32 [2, 1792], P(None, 'tensor'), may hold values from -4 to 4
- probe_lookup_smoothed: float32 [1792, 2, 256], P('dp', None, 'tensor'), may hold values from -0.125 to 0.125
- value_gate_mean: float32 [1792, 2, 1792], P('dp', None, 'tensor'), may hold values from -0.125 to 0.125
- conv_taps_mean: float32 [4, 1792], P(None, 'tensor'), may hold values from -3 to 3
- output_weight_mean: float32 [1792, 1792], P('tensor', 'dp'), may hold values from -3 to 3
- gate_up_mean: float32 [1792, 2, 4096], P('dp', None, 'tensor'), may hold values from -0.125 to 0.125
- down_weight_mean: float32 [4096, 1792], P('tensor', 'dp'), may hold values from -0.09375 to 0.09375
Outputs:
- mixed: bfloat16 [2048, 1792], P('dp', 'tensor')
- input_grad: float32 [2048, 1792], P('dp', 'tensor')
- gains_grad: float32 [2, 1792], P(None, 'tensor')
- query_key_grad: float32 [1792, 2, 256], P('dp', None, 'tensor')
- value_gate_grad: float32 [1792, 2, 1792], P('dp', None, 'tensor')
- conv_taps_grad: float32 [4, 1792], P(None, 'tensor')
- output_weight_grad: float32 [1792, 1792], P('tensor', 'dp')
- gate_up_grad: float32 [1792, 2, 4096], P('dp', None, 'tensor')
- down_weight_grad: float32 [4096, 1792], P('tensor', 'dp')
- gains_change: float32 [2, 1792], P(None, 'tensor')
- query_key_change: float32 [1792, 2, 256], P('dp', None, 'tensor')
- value_gate_change: float32 [1792, 2, 1792], P('dp', None, 'tensor')
- conv_taps_change: float32 [4, 1792], P(None, 'tensor')
- output_weight_change: float32 [1792, 1792], P('tensor', 'dp')
- gate_up_change: float32 [1792, 2, 4096], P('dp', None, 'tensor')
- down_weight_change: float32 [4096, 1792], P('tensor', 'dp')
- gains_momentum: float32 [2, 1792], P(None, 'tensor')
- query_key_momentum: float32 [1792, 2, 256], P('dp', None, 'tensor')
- value_gate_momentum: float32 [1792, 2, 1792], P('dp', None, 'tensor')
- conv_taps_momentum: float32 [4, 1792], P(None, 'tensor')
- output_weight_momentum: float32 [1792, 1792], P('tensor', 'dp')
- gate_up_momentum: float32 [1792, 2, 4096], P('dp', None, 'tensor')
- down_weight_momentum: float32 [4096, 1792], P('tensor', 'dp')
- gains_average: float32 [2, 1792], P(None, 'tensor')
- query_key_average: float32 [1792, 2, 256], P('dp', None, 'tensor')
- value_gate_average: float32 [1792, 2, 1792], P('dp', None, 'tensor')
- conv_taps_average: float32 [4, 1792], P(None, 'tensor')
- output_weight_average: float32 [1792, 1792], P('tensor', 'dp')
- gate_up_average: float32 [1792, 2, 4096], P('dp', None, 'tensor')
- down_weight_average: float32 [4096, 1792], P('tensor', 'dp')
Inputs may be any that keep to these rules, and one draw needn't show every extreme that they name: `documents`: within each aligned block of 256 rows the numbers start at 0 and never fall; a document spans at least 64 and at most 256 rows (the last one before padding may be shorter), and the first block holds a single document; each block ends with at least one and fewer than 64 padding rows marked -1, and has no other -1.
All inputs are finite; a program needn't handle non-finite values.
Results may differ from a plain program's by a relative error of at most 0.013.
Values may be sent and summed in bfloat16 or wider, within the bound.
No kernel may reach another device: no remote copies, remote signals or barrier semaphores. Data moves between devices by JAX's collectives and lax.ppermute only.
A program may use at most 192 MiB of HBM per device.

v0:
```python
import math

import jax
import jax.numpy as jnp
from jax import lax
from jax.experimental import pallas as pl
from jax.experimental.pallas import tpu as pltpu
from jax.experimental.layout import Layout, with_layout_constraint
from jax.sharding import PartitionSpec as P

H = 16
F = 16
KERNEL = 4
EXTRA = 16


DP = "dp"
TENSOR = "tensor"

epsilon = 1e-06
momentum_decay = 0.9
learning_rate = 0.001
average_rate = 0.1

BF = jnp.bfloat16
F32 = jnp.float32
SCALE = 1.0 / math.sqrt(F)


def advance(grad, weight, moment, average):
    moment_new = momentum_decay * moment + (1.0 - momentum_decay) * grad
    change = -learning_rate * ((1.0 - momentum_decay) * grad + momentum_decay * moment_new)
    average_new = average + average_rate * (weight.astype(jnp.float32) + change - average)
    return (change, moment_new, average_new)


def shaped(*shape, dtype=F32):
    return jax.ShapeDtypeStruct(shape, dtype)


def whole():
    return pl.BlockSpec(memory_space=pltpu.VMEM)


def scalars():
    return pl.BlockSpec(memory_space=pltpu.SMEM)


def cost(flops, moved):
    return pl.CostEstimate(flops=int(flops), transcendentals=0, bytes_accessed=int(moved))


def dot(left, right, left_dim=1, right_dim=0):
    return lax.dot_general(
        left, right, (((left_dim,), (right_dim,)), ((), ())), preferred_element_type=F32
    )


def slope_of(argument, logistic):
    return logistic * (1.0 + argument * (1.0 - logistic))


def own_bit(bit):
    return (lax.axis_index(DP) >> bit) & 1


def swap_dp(source, bit):
    count = lax.axis_size(DP)
    return lax.ppermute(source, DP, [(k, k ^ (1 << bit)) for k in range(count)])


def swap_tensor(source, distance):
    count = lax.axis_size(TENSOR)
    return lax.ppermute(source, TENSOR, [(k, k ^ distance) for k in range(count)])


def sum_dp(source):
    for bit in range(lax.axis_size(DP).bit_length() - 1):
        source = source + swap_dp(source, bit)
    return source


def place_rows(own, whole_ref, pieces):
    share = pieces[0].shape[0]
    for k, piece in enumerate(pieces):
        at = pl.multiple_of((own ^ k) * share, share)
        whole_ref[pl.ds(at, share), :] = piece[...]


def send_blocks(own, wide_ref, keep_ref, send_refs):
    share = keep_ref.shape[0]
    keep_ref[...] = wide_ref[pl.ds(pl.multiple_of(own * share, share), share), :]
    for k, send_ref in enumerate(send_refs):
        at = pl.multiple_of((own ^ (k + 1)) * share, share)
        send_ref[:share, :] = wide_ref[pl.ds(at, share), :].astype(BF)


def allowed_pairs(columns, lines_ref):
    tokens = columns.shape[0]
    row_index = lax.broadcasted_iota(jnp.int32, (tokens, tokens), 0)
    column_index = lax.broadcasted_iota(jnp.int32, (tokens, tokens), 1)
    return (columns[:, 0:1] == lines_ref[0:1, :]) & (column_index <= row_index)


def weigh(queries, keys, allowed):
    scores = dot(queries, keys, 1, 1) * SCALE
    weights = jnp.where(allowed, 1.0 + scores + 0.5 * scores * scores, 0.0)
    return scores, weights, jnp.sum(weights, axis=1, keepdims=True)


def head_kernel(
    own_ref, packed_ref, wqk_ref, wvg_ref, taps_ref, lines_ref, out_w_ref,
    x_ref, turned_ref, root_ref, gain_ref, qk_ref, vg_ref,
    mixed_ref, attended_ref, gated_ref, keep_ref, *rest,
):
    send_refs, (shift_ref, wide_ref, normed_ref) = rest[:-3], rest[-3:]
    count, rows, tokens = packed_ref.shape
    share = rows - EXTRA
    width = count * share
    total = jnp.zeros((1, tokens), F32)
    for k in range(count):
        block = packed_ref[k, :share, :].astype(F32)
        total = total + jnp.sum(block * block, axis=0, keepdims=True)
    root = lax.rsqrt(total / width + epsilon)
    root_ref[...] = jnp.broadcast_to(root, root_ref.shape)
    for k in range(count):
        first = k * share
        turned = packed_ref[k, share:, :].astype(F32).T
        at = 0
        for piece in range(-(-share // tokens)):
            length = min(tokens, share - at)
            gain_ref[first + at : first + at + length, :] = turned[
                :length, 2 * piece : 2 * piece + 2
            ]
            at += length
        x_ref[first : first + share, :] = packed_ref[k, :share, :]
    for start in range(0, width, 256):
        block = slice(start, start + 256)
        piece = x_ref[block, :].astype(F32) * root * gain_ref[block, 0:1]
        turned_ref[block, :] = piece.astype(BF)
        normed_ref[:, block] = piece.T.astype(BF)
    normed = normed_ref[...]
    for k in range(2):
        vg_ref[k] = dot(normed, wvg_ref[k], 1, 1)
        qk_ref[k] = dot(normed, wqk_ref[k], 1, 1).astype(BF)
    heads = qk_ref.shape[2] // F
    size = share // heads
    taps = taps_ref[...].astype(F32)
    values = vg_ref[0]
    columns = lines_ref[...].T
    shift_ref[0:8, :] = jnp.zeros((8, share), F32)
    shift_ref[8 : 8 + tokens, :] = values
    summed = values * taps[0:1]
    for j in range(1, KERNEL):
        summed = summed + columns[:, j : j + 1] * (
            shift_ref[8 - j : 8 - j + tokens, :] * taps[j : j + 1]
        )
    mixed_ref[...] = summed.astype(BF)
    allowed = allowed_pairs(columns, lines_ref)
    for h in range(heads):
        feats = slice(h * F, (h + 1) * F)
        vals = slice(h * size, (h + 1) * size)
        _, weights, totals = weigh(qk_ref[0, :, feats], qk_ref[1, :, feats], allowed)
        attended_ref[:, vals] = dot((weights / totals).astype(BF), mixed_ref[:, vals])
    gates = vg_ref[1]
    gated = (attended_ref[...] * (gates * jax.nn.sigmoid(gates))).astype(BF)
    gated_ref[...] = gated
    for start in range(0, width, 256):
        wide_ref[start : start + 256, :] = dot(gated, out_w_ref[:, start : start + 256]).T
    send_blocks(own_ref[0], wide_ref, keep_ref, send_refs)


def ffn_kernel(
    own_ref, hidden_ref, gain_ref, gate_up_ref, down_ref, *rest,
):
    width, tokens = hidden_ref.shape
    count = width // rest[0].shape[0]
    cot_pieces, rest = rest[:count], rest[count:]
    cot_ref, turned_ref, root_ref, right_ref, keep_ref = rest[:5]
    send_refs, (normed_ref, wide_ref) = rest[5:-2], rest[-2:]
    step = pl.program_id(0)

    @pl.when(step == 0)
    def _():
        place_rows(own_ref[0], cot_ref, cot_pieces)
        total = jnp.zeros((1, tokens), F32)
        for start in range(0, width, 256):
            block = hidden_ref[start : start + 256, :].astype(F32)
            total = total + jnp.sum(block * block, axis=0, keepdims=True)
        root = lax.rsqrt(total / width + epsilon)
        root_ref[...] = jnp.broadcast_to(root, root_ref.shape)
        for start in range(0, width, 256):
            piece = (
                hidden_ref[start : start + 256, :].astype(F32)
                * root
                * gain_ref[start : start + 256, 1:2]
            )
            turned_ref[start : start + 256, :] = piece.astype(BF)
            normed_ref[:, start : start + 256] = piece.T.astype(BF)
            wide_ref[start : start + 256, :] = jnp.zeros((256, tokens), F32)

    normed = normed_ref[...]
    gate = dot(normed, gate_up_ref[0])
    up = dot(normed, gate_up_ref[1])
    d_act = dot(down_ref[...], cot_ref[...]).T
    logistic = jax.nn.sigmoid(gate)
    silu = gate * logistic
    right_ref[0] = (d_act * up * slope_of(gate, logistic)).astype(BF)
    right_ref[1] = (d_act * silu).astype(BF)
    right_ref[2] = (silu * up).astype(BF)
    for start in range(0, width, 256):
        rows = slice(start, start + 256)
        wide_ref[rows, :] = (
            wide_ref[rows, :]
            + dot(gate_up_ref[0, rows, :], right_ref[0], 1, 1)
            + dot(gate_up_ref[1, rows, :], right_ref[1], 1, 1)
        )

    @pl.when(step == pl.num_programs(0) - 1)
    def _():
        send_blocks(own_ref[0], wide_ref, keep_ref, send_refs)


def feed_kernel(own_ref, act_ref, down_ref, keep_ref, *rest):
    send_refs, (wide_ref,) = rest[:-1], rest[-1:]
    for start in range(0, wide_ref.shape[0], 256):
        wide_ref[start : start + 256, :] = dot(act_ref[0], down_ref[:, start : start + 256]).T
    send_blocks(own_ref[0], wide_ref, keep_ref, send_refs)


def add_kernel(count, *refs):
    keep_ref, arrived = refs[0], refs[1:count]
    out_ref, rounded_ref = refs[-2:]
    total = keep_ref[...]
    for ref in arrived:
        total = total + ref[...].astype(F32)
    out_ref[...] = total
    rounded_ref[...] = total.astype(BF)


def back_kernel(
    own_ref, hidden_ref, root_two_ref, gain_ref, cot_ref, x_ref, root_one_ref,
    out_w_ref, qk_ref, vg_ref, attended_ref, mixed_ref, taps_ref, lines_ref, wqk_ref, wvg_ref,
    gated_ref, *rest,
):
    width, tokens = hidden_ref.shape
    count = width // rest[0].shape[0]
    d_normed_pieces, rest = rest[:count], rest[count:]
    d_hidden_ref, branch_ref, delta_ref, small_ref, keep_ref, line_ref = rest[:6]
    send_refs, rest = rest[6 : 5 + count], rest[5 + count :]
    wide_ref, d_branch_ref, shift_ref, d_mixed_ref, d_normed_ref = rest
    place_rows(own_ref[0], d_normed_ref, d_normed_pieces)
    share = vg_ref.shape[2]
    heads = qk_ref.shape[2] // F
    size = share // heads
    own = own_ref[0]
    columns = lines_ref[...].T
    root_two = root_two_ref[0:1, :]
    total = jnp.zeros((1, tokens), F32)
    for start in range(0, width, 256):
        rows = slice(start, start + 256)
        unit = hidden_ref[rows, :].astype(F32) * root_two
        scaled = d_normed_ref[rows, :].astype(F32) * gain_ref[rows, 1:2]
        total = total + jnp.sum(scaled * unit, axis=0, keepdims=True)
    mean = total / width
    for start in range(0, width, 256):
        rows = slice(start, start + 256)
        unit = hidden_ref[rows, :].astype(F32) * root_two
        scaled = d_normed_ref[rows, :].astype(F32) * gain_ref[rows, 1:2]
        piece = cot_ref[rows, :].astype(F32) + root_two * (scaled - unit * mean)
        wide_ref[rows, :] = piece
        branch_ref[rows, :] = piece.astype(BF)
        d_branch_ref[:, rows] = piece.T.astype(BF)
    d_hidden_ref[...] = wide_ref[pl.ds(pl.multiple_of(own * share, share), share), :]
    d_gated = dot(d_branch_ref[...], out_w_ref[...], 1, 1)
    gates = vg_ref[1]
    logistic = jax.nn.sigmoid(gates)
    d_attended = (d_gated * (gates * logistic)).astype(BF)
    delta_ref[0, :, :share] = (d_gated * attended_ref[...] * slope_of(gates, logistic)).astype(BF)
    shift_ref[8 : 8 + tokens, :] = d_attended.astype(F32)
    allowed = allowed_pairs(columns, lines_ref)
    first = 2 * share
    last = first + 2 * heads * F
    delta_ref[0, :, last : last + share] = gated_ref[...]
    delta_ref[0, :, last + share :] = jnp.zeros((tokens, heads * F), BF)
    for h in range(heads):
        feats = slice(h * F, (h + 1) * F)
        vals = slice(h * size, (h + 1) * size)
        queries, keys = qk_ref[0, :, feats], qk_ref[1, :, feats]
        scores, weights, totals = weigh(queries, keys, allowed)
        probs = weights / totals
        d_att = shift_ref[8 : 8 + tokens, vals].astype(BF)
        d_mixed_ref[:, vals] = dot(probs.T.astype(BF), d_att)
        d_probs = dot(d_att, mixed_ref[:, vals], 1, 1)
        d_weights = (d_probs - jnp.sum(d_probs * probs, axis=1, keepdims=True)) / totals
        d_scores = jnp.where(allowed, d_weights * (1.0 + scores), 0.0)
        d_q = dot(d_scores.astype(BF), keys) * SCALE
        d_k = dot(d_scores.T.astype(BF), queries) * SCALE
        delta_ref[0, :, first + h * F : first + (h + 1) * F] = d_q.astype(BF)
        at = first + heads * F
        delta_ref[0, :, at + h * F : at + (h + 1) * F] = d_k.astype(BF)
    taps = taps_ref[...].astype(F32)
    d_mixed = d_mixed_ref[...]
    values = vg_ref[0]
    small_ref[...] = jnp.zeros(small_ref.shape, F32)
    small_ref[0:1, :] = jnp.sum(d_mixed * values, axis=0, keepdims=True)
    shift_ref[0:8, :] = jnp.zeros((8, share), F32)
    shift_ref[8 : 8 + tokens, :] = values
    for j in range(1, KERNEL):
        masked = columns[:, j : j + 1] * d_mixed
        small_ref[j : j + 1, :] = jnp.sum(
            masked * shift_ref[8 - j : 8 - j + tokens, :], axis=0, keepdims=True
        )
    d_values = d_mixed * taps[0:1]
    shift_ref[8 + tokens : 16 + tokens, :] = jnp.zeros((8, share), F32)
    for j in range(1, KERNEL):
        shift_ref[8 : 8 + tokens, :] = columns[:, j : j + 1] * d_mixed
        d_values = d_values + shift_ref[8 + j : 8 + j + tokens, :] * taps[j : j + 1]
    delta_ref[0, :, share : 2 * share] = d_values.astype(BF)
    d_gates = delta_ref[0, :, :share]
    d_values = delta_ref[0, :, share : 2 * share]
    d_queries = delta_ref[0, :, first : first + heads * F]
    d_keys = delta_ref[0, :, first + heads * F : first + 2 * heads * F]
    root_one = root_one_ref[0:1, :]
    line = jnp.zeros((1, tokens), F32)
    for start in range(0, width, 256):
        rows = slice(start, start + 256)
        piece = (
            dot(d_queries, wqk_ref[0, :, rows])
            + dot(d_keys, wqk_ref[1, :, rows])
            + dot(d_values, wvg_ref[0, :, rows])
            + dot(d_gates, wvg_ref[1, :, rows])
        ).T
        wide_ref[rows, :] = piece
        unit = x_ref[rows, :].astype(F32) * root_one
        line = line + jnp.sum(piece * (unit * gain_ref[rows, 0:1]), axis=0, keepdims=True)
    line_ref[...] = jnp.broadcast_to(line, line_ref.shape)
    send_blocks(own, wide_ref, keep_ref, send_refs)
    high = line.astype(BF)
    low = (line - high.astype(F32)).astype(BF)
    index = lax.broadcasted_iota(jnp.int32, (EXTRA, tokens), 0)
    extra = jnp.where(
        index == 0,
        jnp.broadcast_to(high.astype(F32), (EXTRA, tokens)),
        jnp.where(index == 1, jnp.broadcast_to(low.astype(F32), (EXTRA, tokens)), 0.0),
    ).astype(BF)
    for send_ref in send_refs:
        send_ref[share:, :] = extra


def merged(source):
    rows, columns = source.shape[-2:]
    return source.reshape(-1, rows, columns) if rows % 16 else source.reshape(1, -1, columns)


def product(lefts, rights, column, out_ref, at, size):
    sources = [merged(left) for left in lefts]
    rows = out_ref.shape[1]
    for k in range(sources[0].shape[0]):
        blocks = slice(None) if sources[0].shape[0] == 1 else slice(k, k + 1)
        value = dot(sources[0][k], rights[0][:, column : column + size])
        for source, right in zip(sources[1:], rights[1:]):
            value = value + dot(source[k], right[:, column : column + size])
        out_ref[blocks, :, at : at + size] = value.reshape(-1, rows, size).astype(BF)


def stage_kernel(orders, tile, where_ref, *refs):
    pairs, rights, outs = (refs[0:2], refs[2:4]), refs[4:6], refs[6:]
    per_slab = rights[0].shape[2]
    for p, order in enumerate(orders):
        for start in range(0, 3 * tile, 256):
            column = 3 * p * tile + start
            late = column >= 4 * tile
            lefts = [
                left[:, where_ref[1 + p], :, where_ref[0]]
                for left in (view_of(ref, order) for ref in pairs[int(late)])
            ]
            slab = [right[column // per_slab] for right in rights]
            product(lefts, slab, column % per_slab, outs[p], start, min(256, 3 * tile))


def view_of(ref, order):
    half, pair, rows, tokens = ref.shape
    low = 1 << (order[0] - 1)
    return ref.reshape(half // 2 // low, 2, low, pair, rows, tokens)


def path_orders(bits):
    return [list(range(1, bits)), list(reversed(range(1, bits)))]


def sum_rows(lefts, rights, tile, keep):
    count = lax.axis_size(DP)
    bits = count.bit_length() - 1
    width, tokens = lefts[0][0].shape
    rows = width // count
    orders = path_orders(bits)
    places = [own_bit(order[0]) for order in orders]
    if not keep:
        places = [1 - place for place in places]
    where = jnp.stack([own_bit(0)] + places).astype(jnp.int32)
    operands = [left.reshape(count // 2, 2, rows, tokens) for pair in lefts for left in pair]
    return pl.pallas_call(
        lambda *refs: stage_kernel(orders, tile, *refs),
        out_shape=[shaped(count // 4, rows, 3 * tile, dtype=BF)] * 2,
        in_specs=[scalars()] + [whole()] * 6,
        cost_estimate=cost(6 * width * tokens * tile, 6 * width * tile),
    )(where, *operands, *rights)


def third_kernel(count, where_ref, *refs):
    for p in range(count):
        kept, more = refs[2 * p : 2 * p + 2]
        outs = refs[2 * count + 2 * p : 2 * count + 2 * p + 2]
        for which, out_ref in enumerate(outs):
            place = where_ref[2 * p + which]
            total = kept[:, place].astype(F32) + more[:, place].astype(F32)
            out_ref[...] = total.astype(BF).reshape(out_ref.shape)


def sum_rows_third(sends, keeps):
    bits = lax.axis_size(DP).bit_length() - 1
    orders = path_orders(bits)
    remaining = [[bit for bit in reversed(range(1, bits)) if bit != order[0]] for order in orders]
    arrived = [swap_dp(send, order[0]) for order, send in zip(orders, sends)]
    for stage in range(1, bits - 1):
        operands, out_shape, places = [], [], []
        moved = 0
        for p, order in enumerate(orders):
            at = remaining[p].index(order[stage])
            low = 1 << (len(remaining[p]) - 1 - at)
            blocks, rows, size = keeps[p].shape
            high = blocks // (2 * low)
            remaining[p].pop(at)
            bit = own_bit(order[stage])
            places += [1 - bit, bit]
            operands += [each.reshape(high, 2, low, rows, size) for each in (keeps[p], arrived[p])]
            out_shape += [shaped(high * low, rows, size, dtype=BF)] * 2
            moved += 6 * blocks * rows * size
        outs = pl.pallas_call(
            lambda *refs: third_kernel(len(orders), *refs),
            out_shape=out_shape,
            in_specs=[scalars()] + [whole()] * len(operands),
            cost_estimate=cost(moved, moved),
        )(jnp.stack(places).astype(jnp.int32), *operands)
        sends, keeps = outs[0::2], outs[1::2]
        arrived = [swap_dp(send, order[stage]) for order, send in zip(orders, sends)]
    return [
        (keep.reshape(keep.shape[1:]), piece.reshape(piece.shape[1:]))
        for keep, piece in zip(keeps, arrived)
    ]


def advance_kernel(units, split, *refs):
    keep_a, more_a, keep_b, more_b, weight_ref, moment_ref, mean_ref = refs[:7]
    grad_ref, change_ref, moment_out_ref, mean_out_ref = refs[7:]
    rows = keep_a.shape[0]
    tiles = units // 128
    for column in range(0, 2 * units, 128):
        if column < units + split:
            tile = slice(column, column + 128)
            value = keep_a[:, tile].astype(F32) + more_a[:, tile].astype(F32)
        else:
            tile = slice(column - units - split, column - units - split + 128)
            value = keep_b[:, tile].astype(F32) + more_b[:, tile].astype(F32)
        at = (column % units) // 128 * 2 + column // units
        grad_ref[pl.ds(at, rows, stride=2 * tiles), :] = value
    change, moment, mean = advance(
        grad_ref[...], weight_ref[...], moment_ref[...], mean_ref[...]
    )
    change_ref[...] = change
    moment_out_ref[...] = moment
    mean_out_ref[...] = mean


def flattened(source):
    rows, pair, units = source.shape
    tiles = source.reshape(rows, pair, units // 128, 128).transpose(0, 2, 1, 3)
    return tiles.reshape(-1, 128)


def unflattened(source, units):
    tiles = source.reshape(-1, units // 128, 2, 128).transpose(0, 2, 1, 3)
    return tiles.reshape(-1, 2, units)


def advance_pairs(path_a, path_b, split, weight, moment, mean):
    rows, _, units = moment.shape
    step = 112 if rows % 112 == 0 else rows
    width = path_a[0].shape[1]
    flat = step * 2 * units // 128
    spec = pl.BlockSpec((flat, 128), lambda k: (k, 0))
    outs = pl.pallas_call(
        lambda *refs: advance_kernel(units, split, *refs),
        out_shape=[shaped(rows * 2 * units // 128, 128) for _ in range(4)],
        grid=(rows // step,),
        in_specs=[pl.BlockSpec((step, width), lambda k: (k, 0))] * 2
        + [pl.BlockSpec((step, units - split), lambda k: (k, 0))] * 2
        + [spec] * 3,
        out_specs=[spec] * 4,
        cost_estimate=cost(10 * rows * units, 64 * rows * units),
        name="adv",
    )(*path_a, *path_b, flattened(weight.astype(F32)), flattened(moment), flattened(mean))
    return [unflattened(out, units) for out in outs]


def last_kernel(share, width, *refs):
    keep_a, more_a, keep_b, more_b = refs[:4]
    pair_in, qk_in, out_in = refs[4:7], refs[7:10], refs[10:13]
    pair_out, qk_out, out_out = refs[13:17], refs[17:21], refs[21:25]
    whole_ref = refs[25]
    half = keep_a.shape[1]
    whole_ref[:, :half] = keep_a[...].astype(F32) + more_a[...].astype(F32)
    whole_ref[:, half:] = keep_b[...].astype(F32) + more_b[...].astype(F32)

    def step(grad, inputs, outputs, index):
        change, moment, mean = advance(grad, *(each[index] for each in inputs))
        for ref, value in zip(outputs, (grad, change, moment, mean)):
            ref[index] = value

    everything = (slice(None), slice(None))
    for which, start in ((0, share), (1, 0)):
        step(
            whole_ref[:, start : start + share], pair_in, pair_out,
            (slice(None), which, slice(None)),
        )
    first = 2 * share
    step(whole_ref[:, first : first + width].T, qk_in, qk_out, everything)
    first += width
    step(whole_ref[:, first : first + share].T, out_in, out_out, everything)


def local(
    inputs,
    cotangent,
    documents,
    gains,
    query_key,
    value_gate,
    conv_taps,
    output_weight,
    gate_up,
    down_weight,
    gains_moment,
    query_key_moment,
    value_gate_moment,
    conv_taps_moment,
    output_weight_moment,
    gate_up_moment,
    down_weight_moment,
    gains_mean,
    probe_lookup_smoothed,
    value_gate_mean,
    conv_taps_mean,
    output_weight_mean,
    gate_up_mean,
    down_weight_mean,
):
    tokens, share = inputs.shape
    groups = lax.axis_size(TENSOR)
    width = share * groups
    heads = H // groups
    key_width = heads * F
    hidden_units = down_weight.shape[0]
    own = lax.axis_index(TENSOR)
    own_index = own.astype(jnp.int32).reshape(1)

    inputs_turned = inputs.T
    pieces = -(-share // tokens)
    gain_lines = jnp.pad(gains, ((0, 0), (0, pieces * tokens - share)))
    gain_lines = gain_lines.reshape(2, pieces, tokens).transpose(1, 0, 2).reshape(-1, tokens)
    packed = jnp.concatenate(
        [inputs_turned, jnp.pad(gain_lines, ((0, EXTRA - 2 * pieces), (0, 0)))], axis=0
    )
    packed_whole = lax.all_gather(packed, TENSOR)
    documents_column = documents[:, None]
    lines = [documents.astype(F32)]
    for offset in range(1, KERNEL):
        earlier = jnp.pad(documents, (offset, 0), constant_values=-2)[:tokens]
        lines.append((earlier == documents).astype(F32))
    lines = jnp.pad(jnp.stack(lines), ((0, 8 - KERNEL), (0, 0)))
    masked = jnp.where(documents_column >= 0, cotangent, jnp.zeros_like(cotangent)).T
    masked, packed_whole = lax.optimization_barrier((masked, packed_whole))

    def sends(extra=0):
        return [shaped(share + extra, tokens, dtype=BF) for _ in range(groups - 1)]

    vmem = whole()
    query_key_rows = jnp.transpose(query_key, (1, 2, 0))
    value_gate_rows = jnp.transpose(value_gate, (1, 2, 0))
    cot_pieces = [masked] + [swap_tensor(masked, k) for k in range(1, groups)]
    (
        x_turned, normed_turned, root_one, gain_columns, projected, mixing,
        mixed_values, attended, gated, branch_keep, *branch_sends,
    ) = pl.pallas_call(
        head_kernel,
        out_shape=[
            shaped(width, tokens, dtype=BF),
            shaped(width, tokens, dtype=BF),
            shaped(8, tokens),
            shaped(width, 2),
            shaped(2, tokens, key_width, dtype=BF),
            shaped(2, tokens, share),
            shaped(tokens, share, dtype=BF),
            shaped(tokens, share),
            shaped(tokens, share, dtype=BF),
            shaped(share, tokens),
        ]
        + sends(),
        in_specs=[scalars()] + [vmem] * 6,
        scratch_shapes=[
            pltpu.VMEM((tokens + 16, share), F32),
            pltpu.VMEM((width, tokens), F32),
            pltpu.VMEM((tokens, width), BF),
        ],
        cost_estimate=cost(7 * tokens * share * width, 10 * share * width),
        name="head",
    )(
        own_index, packed_whole, query_key_rows, value_gate_rows, conv_taps, lines,
        output_weight,
    )
    normed_pair = (normed_turned, swap_dp(normed_turned, 0))
    arrived = [swap_tensor(send, k + 1) for k, send in enumerate(branch_sends)]
    gate_up_split = jnp.transpose(gate_up, (1, 0, 2))
    middle = hidden_units // 2
    dp_index = lax.axis_index(DP)
    dp_count = lax.axis_size(DP)

    def own_rows(source, axis_dim):
        length = source.shape[axis_dim] // dp_count
        return lax.dynamic_slice_in_dim(source, dp_index * length, length, axis_dim)

    own_weights = (
        own_rows(query_key, 0).astype(F32),
        own_rows(value_gate, 0).astype(F32),
        own_rows(output_weight, 1).astype(F32),
        own_rows(gate_up, 0).astype(F32),
        own_rows(down_weight, 1).astype(F32),
    )
    own_weights, branch_keep = lax.optimization_barrier((own_weights, branch_keep))
    own_query_key, own_value_gate, own_output_weight, own_gate_up, own_down_weight = own_weights
    hidden_own = inputs_turned.astype(F32) + branch_keep
    for piece in arrived:
        hidden_own = hidden_own + piece.astype(F32)
    hidden = lax.all_gather(hidden_own.astype(BF), TENSOR, axis=0, tiled=True)

    tile = 256
    cot_turned, normed_two_turned, root_two, ffn_right, keep_two, *sends_two = pl.pallas_call(
        ffn_kernel,
        out_shape=[
            shaped(width, tokens, dtype=BF),
            shaped(width, tokens, dtype=BF),
            shaped(8, tokens),
            shaped(3, tokens, hidden_units, dtype=BF),
            shaped(share, tokens),
        ]
        + sends(),
        grid=(hidden_units // tile,),
        in_specs=[
            scalars(),
            pl.BlockSpec((width, tokens), lambda f: (0, 0)),
            pl.BlockSpec((width, 2), lambda f: (0, 0)),
            pl.BlockSpec((2, width, tile), lambda f: (0, 0, f)),
            pl.BlockSpec((tile, width), lambda f: (f, 0)),
        ]
        + [pl.BlockSpec((share, tokens), lambda f: (0, 0))] * groups,
        out_specs=[
            pl.BlockSpec((width, tokens), lambda f: (0, 0)),
            pl.BlockSpec((width, tokens), lambda f: (0, 0)),
            pl.BlockSpec((8, tokens), lambda f: (0, 0)),
            pl.BlockSpec((3, tokens, tile), lambda f: (0, 0, f)),
            pl.BlockSpec((share, tokens), lambda f: (0, 0)),
        ]
        + [pl.BlockSpec((share, tokens), lambda f: (0, 0)) for _ in range(groups - 1)],
        scratch_shapes=[pltpu.VMEM((tokens, width), BF), pltpu.VMEM((width, tokens), F32)],
        cost_estimate=cost(10 * tokens * width * hidden_units, 6 * width * hidden_units),
        name="ffn",
    )(own_index, hidden, gain_columns, gate_up_split, down_weight, *cot_pieces)
    arrived_two = [swap_tensor(send, k + 1) for k, send in enumerate(sends_two)]

    middle = hidden_units // 2
    ffn_pairs = [(each, swap_dp(each, 0)) for each in (normed_two_turned, cot_turned, ffn_right)]
    ffn_group = (ffn_pairs[:2], ffn_pairs[2], hidden_units // 2)
    ffn_sends = sum_rows(*ffn_group, False)
    ffn_keeps = sum_rows(*ffn_group, True)

    d_normed_two_own, d_normed_two_rounded = pl.pallas_call(
        lambda *refs: add_kernel(groups, *refs),
        out_shape=[shaped(share, tokens), shaped(share, tokens, dtype=BF)],
        in_specs=[vmem] * groups + [pl.BlockSpec(memory_space=pl.ANY)] * 2,
        cost_estimate=cost(4 * share * tokens, 14 * share * tokens),
        name="add",
    )(keep_two, *arrived_two, *ffn_sends)
    d_normed_two_pieces = [d_normed_two_rounded] + [
        swap_tensor(d_normed_two_rounded, k) for k in range(1, groups)
    ]
    ffn_rows = sum_rows_third(ffn_sends, ffn_keeps)
    feed_keep, *feed_sends = pl.pallas_call(
        feed_kernel,
        out_shape=[shaped(share, tokens)] + sends(),
        grid=(1,),
        in_specs=[
            scalars(),
            pl.BlockSpec((1, tokens, hidden_units), lambda k: (2, 0, 0)),
            pl.BlockSpec((hidden_units, width), lambda k: (0, 0)),
        ],
        out_specs=[pl.BlockSpec((share, tokens), lambda k: (0, 0))] * groups,
        scratch_shapes=[pltpu.VMEM((width, tokens), F32)],
        cost_estimate=cost(2 * tokens * width * hidden_units, 2 * width * hidden_units),
        name="feed",
    )(own_index, ffn_right, down_weight)

    d_hidden_own, d_branch_turned, delta, taps_part, keep_one, line_one, *sends_one = (
        pl.pallas_call(
            back_kernel,
            out_shape=[
                shaped(share, tokens),
                shaped(width, tokens, dtype=BF),
                shaped(1, tokens, 3 * (share + key_width), dtype=BF),
                shaped(8, share),
                shaped(share, tokens),
                shaped(8, tokens),
            ]
            + sends(EXTRA),
            in_specs=[scalars()] + [vmem] * (16 + groups),
            scratch_shapes=[
                pltpu.VMEM((width, tokens), F32),
                pltpu.VMEM((tokens, width), BF),
                pltpu.VMEM((tokens + 16, share), F32),
                pltpu.VMEM((tokens, share), F32),
                pltpu.VMEM((width, tokens), BF),
            ],
            cost_estimate=cost(8 * tokens * width * share, 20 * width * share),
            name="back",
        )(
            own_index, hidden, root_two, gain_columns, cot_turned, x_turned,
            root_one, output_weight, projected, mixing, attended, mixed_values, conv_taps, lines,
            query_key_rows, value_gate_rows, gated, *d_normed_two_pieces,
        )
    )
    arrived_one = [swap_tensor(send, k + 1) for k, send in enumerate(sends_one)]
    all_columns = 2 * (share + key_width)
    mix_pairs = [normed_pair] + [(each, swap_dp(each, 0)) for each in (d_branch_turned, delta)]
    mix_group = (mix_pairs[:2], mix_pairs[2], all_columns // 4)
    mix_sends = sum_rows(*mix_group, False)
    mix_keeps = sum_rows(*mix_group, True)
    mix_rows = sum_rows_third(mix_sends, mix_keeps)

    feed_own = feed_keep
    feed_arrived = [swap_tensor(send, k + 1) for k, send in enumerate(feed_sends)]
    for piece in feed_arrived:
        feed_own = feed_own + piece.astype(F32)
    mixed = (hidden_own + feed_own).astype(BF).T

    def own_rows_of(source):
        return lax.dynamic_slice_in_dim(source, own * share, share, 0)

    gain_own = gains.astype(F32).T
    root_one_line, root_two_line = root_one[0:1], root_two[0:1]
    unit_two_own = own_rows_of(hidden).astype(F32) * root_two_line
    gain_two_grad = jnp.sum(d_normed_two_own * unit_two_own, axis=1)
    d_normed_own, line = keep_one, line_one[0:1]
    for piece in arrived_one:
        d_normed_own = d_normed_own + piece[:share].astype(F32)
        line = line + (piece[share : share + 1].astype(F32) + piece[share + 1 : share + 2].astype(F32))
    unit_one_own = inputs_turned.astype(F32) * root_one_line
    input_grad = (
        d_hidden_own
        + root_one_line * (d_normed_own * gain_own[:, 0:1] - unit_one_own * (line / width))
    ).T
    gain_one_grad = jnp.sum(d_normed_own * unit_one_own, axis=1)
    small = sum_dp(
        jnp.concatenate(
            [gain_one_grad[None], gain_two_grad[None], taps_part[:KERNEL], jnp.zeros((2, share))],
            axis=0,
        )
    )
    gains_grad = small[:2]
    conv_taps_grad = small[2 : 2 + KERNEL]
    down_weight_grad = sum(part[:, middle:].astype(F32) for part in ffn_rows[1]).T
    down_weight_grad = with_layout_constraint(
        lax.optimization_barrier(down_weight_grad), Layout(major_to_minor=(1, 0))
    )
    rows = width // lax.axis_size(DP)

    def turned_pairs(source):
        return source.transpose(1, 2, 0).reshape(2 * key_width, rows)

    last = pl.pallas_call(
        lambda *refs: last_kernel(share, 2 * key_width, *refs),
        out_shape=[shaped(rows, 2, share)] * 4
        + [shaped(2 * key_width, rows)] * 4
        + [shaped(share, rows)] * 4,
        in_specs=[vmem] * 13,
        scratch_shapes=[pltpu.VMEM((rows, 3 * (share + key_width)), F32)],
        cost_estimate=cost(30 * rows * share, 100 * rows * share),
        name="last",
    )(
        *mix_rows[0], *mix_rows[1],
        own_value_gate, value_gate_moment, value_gate_mean,
        turned_pairs(own_query_key), turned_pairs(query_key_moment),
        turned_pairs(probe_lookup_smoothed),
        own_output_weight, output_weight_moment, output_weight_mean,
    )
    value_gate_grad, value_gate_change, value_gate_momentum, value_gate_average = last[:4]
    query_key_grad, query_key_change, query_key_momentum, query_key_average = [
        each.reshape(2, key_width, rows).transpose(2, 0, 1) for each in last[4:8]
    ]
    (
        output_weight_grad, output_weight_change, output_weight_momentum,
        output_weight_average,
    ) = last[8:]
    gains_change, gains_momentum, gains_average = advance(
        gains_grad, gains, gains_moment, gains_mean
    )
    conv_taps_change, conv_taps_momentum, conv_taps_average = advance(
        conv_taps_grad, conv_taps, conv_taps_moment, conv_taps_mean
    )
    gate_up_grad, gate_up_change, gate_up_momentum, gate_up_average = advance_pairs(
        *ffn_rows, middle, own_gate_up, gate_up_moment, gate_up_mean
    )
    down_weight_change, down_weight_momentum, down_weight_average = advance(
        down_weight_grad, own_down_weight, down_weight_moment, down_weight_mean
    )
    return (
        mixed,
        input_grad,
        gains_grad,
        query_key_grad,
        value_gate_grad,
        conv_taps_grad,
        output_weight_grad,
        gate_up_grad,
        down_weight_grad,
        gains_change,
        query_key_change,
        value_gate_change,
        conv_taps_change,
        output_weight_change,
        gate_up_change,
        down_weight_change,
        gains_momentum,
        query_key_momentum,
        value_gate_momentum,
        conv_taps_momentum,
        output_weight_momentum,
        gate_up_momentum,
        down_weight_momentum,
        gains_average,
        query_key_average,
        value_gate_average,
        conv_taps_average,
        output_weight_average,
        gate_up_average,
        down_weight_average,
    )


def solution(mesh):
    return jax.shard_map(
        local,
        mesh=mesh,
        in_specs=(
            P(DP, TENSOR),
            P(DP, TENSOR),
            P(DP),
            P(None, TENSOR),
            P(None, None, TENSOR),
            P(None, None, TENSOR),
            P(None, TENSOR),
            P(TENSOR, None),
            P(None, None, TENSOR),
            P(TENSOR, None),
            P(None, TENSOR),
            P(DP, None, TENSOR),
            P(DP, None, TENSOR),
            P(None, TENSOR),
            P(TENSOR, DP),
            P(DP, None, TENSOR),
            P(TENSOR, DP),
            P(None, TENSOR),
            P(DP, None, TENSOR),
            P(DP, None, TENSOR),
            P(None, TENSOR),
            P(TENSOR, DP),
            P(DP, None, TENSOR),
            P(TENSOR, DP),
        ),
        out_specs=(
            P(DP, TENSOR),
            P(DP, TENSOR),
            P(None, TENSOR),
            P(DP, None, TENSOR),
            P(DP, None, TENSOR),
            P(None, TENSOR),
            P(TENSOR, DP),
            P(DP, None, TENSOR),
            P(TENSOR, DP),
            P(None, TENSOR),
            P(DP, None, TENSOR),
            P(DP, None, TENSOR),
            P(None, TENSOR),
            P(TENSOR, DP),
            P(DP, None, TENSOR),
            P(TENSOR, DP),
            P(None, TENSOR),
            P(DP, None, TENSOR),
            P(DP, None, TENSOR),
            P(None, TENSOR),
            P(TENSOR, DP),
            P(DP, None, TENSOR),
            P(TENSOR, DP),
            P(None, TENSOR),
            P(DP, None, TENSOR),
            P(DP, None, TENSOR),
            P(None, TENSOR),
            P(TENSOR, DP),
            P(DP, None, TENSOR),
            P(TENSOR, DP),
        ),
        check_vma=False,
    )
```

profile of v0, /device:TPU:0, one launch (start us, length us, event | category | flops | bytes accessed | tf_op | source)
XLA Modules:
  0.0 274.2 jit_solution(12471524556219171025)
XLA Ops:
  3.3 23.5 %all-gather = bf16[1856,256]{1,0:T(8,128)(2,1)} all-gather(bf16[464,256]{1,0:T(8,128)(2,1)S(1)} %fusion.11), channel_id=2, replica_groups=mesh['dp'=8,'tensor'=4] {'tensor'}, dimensions={0}, use_global_device_ids=true | all-gather | bytes 1187840 | tf_op jit(solution)/shard_map/all_gather | solution.py:575
  27.9 2.3 collective-permute-start.4
  30.8 8.0 %head.1 = (bf16[1792,256]{1,0:T(8,128)(2,1)}, bf16[1792,256]{1,0:T(8,128)(2,1)}, f32[8,256]{1,0:T(8,128)}, f32[1792,2]{1,0:T(8,128)}, bf16[2,256,64]{2,1,0:T(8,1...) custom-call(s32[1]{0:T(128)} %bitcast.1.own_ref, ...), custom_call_target="tpu_custom_call" | custom-call | flops 1438646272 | bytes 8028160 | tf_op jit(solution)/shard_map/head/pallas_call | solution.py:595
  38.8 2.0 collective-permute-start.2
  40.9 2.4 collective-permute-start
  44.5 1.9 dynamic-slice_convert_fusion.1.refs_10_
  50.0 8.3 %copy.68 = bf16[1792,2,1024]{2,0,1:T(8,128)(2,1)} copy(bf16[1792,2,1024]{2,1,0:T(2,128)(2,1)} %param.32) | data formatting | bytes 14680064 | tf_op args[8]
  58.3 1.7 dynamic-slice_convert_fusion.2
  60.0 3.1 %dynamic-slice_convert_fusion = f32[224,2,1024]{2,1,0:T(2,128)} fusion(bf16[1792,2,1024]{2,1,0:T(2,128)(2,1)} %param.32, s32[]{:T(128)S(6)} %select_n.14), kind=kLoop, calls=%fused_computation.5 | loop fusion | flops 458752 | bytes 2752516 | tf_op jit(solution)/shard_map/convert_element_type | solution.py:637
  63.1 2.0 collective-permute-start.5
  65.3 23.3 %all_gather.11.hidden_ref = bf16[1792,256]{1,0:T(8,128)(2,1)} all-gather(bf16[448,256]{1,0:T(8,128)(2,1)S(1)} %fusion.24), channel_id=1, replica_groups=mesh['dp'=8,'tensor'=4] {'tensor'}, dimensions={0}, use_global_device_ids=true | all-gather | bytes 1146880 | tf_op jit(solution)/shard_map/all_gather | solution.py:645
  89.4 13.3 %ffn.1 = (bf16[1792,256]{1,0:T(8,128)(2,1)}, bf16[1792,256]{1,0:T(8,128)(2,1)}, f32[8,256]{1,0:T(8,128)}, bf16[3,256,1024]{2,1,0:T(8,128)(2,1)}, f32[448,256]{1,...) custom-call(s32[1]{0:T(128)} %bitcast.1.own_ref, ...), custom_call_target="tpu_custom_call" | custom-call | flops 4697620480 | bytes 11010048 | tf_op jit(solution)/shard_map/ffn/pallas_call | solution.py:648
  103.4 1.8 collective-permute-start.9
  105.2 2.7 collective-permute-start.10
  107.9 3.9 %collective-permute-start.11 = (bf16[448,256]{1,0:T(8,128)(2,1)}, bf16[448,256]{1,0:T(8,128)(2,1)}, u32[]{:S(2)}, u32[]{:S(2)}) collective-permute-start(bf16[448,256]{1,0:T(8,128)(2,1)} %get-tuple-element.131), channel_id=1, source_target_pairs={{0,3},{1,2},{2,1},{3,0},{4,7},{5,6},{6,5},{7,4},{8,11},{9,10},{10,... | collective-permute-start | bytes 688136 | tf_op jit(solution)/shard_map/ppermute | solution.py:74
  113.6 5.7 %shard_map.463 = (bf16[2,224,1536]{2,1,0:T(8,128)(2,1)}, bf16[2,224,1536]{2,1,0:T(8,128)(2,1)}) custom-call(s32[3]{0:T(128)} %pad_add_fusion.refs_0_, bf16[4,2,224,256]{3,2,1,0:T(8,128)(2,1)} %bitcast.133, bf16[4,2,224,256]{3,2,1,0:T(8,128)(2,1)} %bitcast.18.refs_2_, bf16[4,2,224,256]{3,2,1,0:T(8,128)(2,1)} %bitcast.125, ...), custom_call_target="tpu_custom_call" | custom-call | flops 1409286144 | bytes 5505024 | tf_op jit(solution)/shard_map/pallas_call | solution.py:403
  119.3 5.5 %collective-permute-done.10.refs_2_ = bf16[448,256]{1,0:T(8,128)(2,1)} collective-permute-done((bf16[448,256]{1,0:T(8,128)(2,1)}, bf16[448,256]{1,0:T(8,128)(2,1)}, u32[]{:S(2)}, u32[]{:S(2)}) %collective-permute-start.10) | collective-permute-done | bytes 229408 | tf_op jit(solution)/shard_map/ppermute | solution.py:74
  124.8 2.3 add.295
  127.1 4.7 %collective-permute-start.15 = (bf16[448,256]{1,0:T(8,128)(2,1)}, bf16[448,256]{1,0:T(8,128)(2,1)S(1)}, u32[]{:S(2)}, u32[]{:S(2)}) collective-permute-start(bf16[448,256]{1,0:T(8,128)(2,1)} %get-tuple-element.135.rest_0_), channel_id=1, source_target_pairs={{0,1},{1,0},{2,3},{3,2},{4,5},{5,4},{6,7},{7,6},{8,9},{9,8},{10,11... | collective-permute-start | bytes 688136 | tf_op jit(solution)/shard_map/ppermute | solution.py:74
  132.6 1.5 collective-permute-start.17
  134.1 6.9 %collective-permute-done.15.rest_1_ = bf16[448,256]{1,0:T(8,128)(2,1)S(1)} collective-permute-done((bf16[448,256]{1,0:T(8,128)(2,1)}, bf16[448,256]{1,0:T(8,128)(2,1)S(1)}, u32[]{:S(2)}, u32[]{:S(2)}) %collective-permute-start.15) | collective-permute-done | bytes 229408 | tf_op jit(solution)/shard_map/ppermute | solution.py:74
  141.0 10.1 %collective-permute-done.16.rest_2_ = bf16[448,256]{1,0:T(8,128)(2,1)S(1)} collective-permute-done((bf16[448,256]{1,0:T(8,128)(2,1)}, bf16[448,256]{1,0:T(8,128)(2,1)S(1)}, u32[]{:S(2)}, u32[]{:S(2)}) %collective-permute-start.16) | collective-permute-done | bytes 229408 | tf_op jit(solution)/shard_map/ppermute | solution.py:74
  151.9 13.3 %back.1 = (f32[448,256]{1,0:T(8,128)}, bf16[1792,256]{1,0:T(8,128)(2,1)}, bf16[1,256,1536]{2,1,0:T(8,128)(2,1)}, f32[8,448]{1,0:T(8,128)}, f32[448,256]{1,0:T(8,...) custom-call(s32[1]{0:T(128)} %bitcast.1.own_ref, ...), custom_call_target="tpu_custom_call" | custom-call | flops 1644167168 | bytes 16056320 | tf_op jit(solution)/shard_map/back/pallas_call | solution.py:714
  165.2 2.4 collective-permute-start.20
  167.6 2.7 collective-permute-start.19
  172.0 1.5 collective-permute-start.31
  175.4 1.6 collective-permute-start.32
  176.9 10.5 %collective-permute-done.19 = bf16[464,256]{1,0:T(8,128)(2,1)} collective-permute-done((bf16[464,256]{1,0:T(8,128)(2,1)}, bf16[464,256]{1,0:T(8,128)(2,1)}, u32[]{:S(2)}, u32[]{:S(2)}) %collective-permute-start.19) | collective-permute-done | bytes 237600 | tf_op jit(solution)/shard_map/ppermute | solution.py:74
  188.3 2.5 fusion.7
  193.2 1.5 collective-permute-start.22
  194.7 4.5 %feed.1 = (f32[448,256]{1,0:T(8,128)}, bf16[448,256]{1,0:T(8,128)(2,1)}, bf16[448,256]{1,0:T(8,128)(2,1)}, bf16[448,256]{1,0:T(8,128)(2,1)}) custom-call(s32[1]{0:T(128)} %bitcast.1.own_ref, bf16[3,256,1024]{2,1,0:T(8,128)(2,1)} %get-tuple-element.114.act_ref.refs_5_, bf16[1024,1792]{1,0:T(8,128)(2,1)} %down_ref.3), custom_call_target="tpu_custom_call" | custom-call | flops 939524096 | bytes 3670016 | tf_op jit(solution)/shard_map/feed/pallas_call | solution.py:698
  199.2 3.4 %collective-permute-done.22 = f32[8,448]{1,0:T(8,128)S(1)} collective-permute-done((f32[8,448]{1,0:T(8,128)S(1)}, f32[8,448]{1,0:T(8,128)S(1)}, u32[]{:S(2)}, u32[]{:S(2)}) %collective-permute-start.22) | collective-permute-done | bytes 14368 | tf_op jit(solution)/shard_map/ppermute | solution.py:69
  202.6 2.4 collective-permute-start.8
  207.6 6.0 %shard_map.467 = (bf16[2,224,1536]{2,1,0:T(8,128)(2,1)}, bf16[2,224,1536]{2,1,0:T(8,128)(2,1)}) custom-call(s32[3]{0:T(128)} %pad_add_fusion.2.refs_0_, bf16[4,2,224,256]{3,2,1,0:T(8,128)(2,1)} %bitcast.134, bf16[4,2,224,256]{3,2,1,0:T(8,128)(2,1)} %bitcast.18.refs_2_, bf16[4,2,224,256]{3,2,1,0:T(8,128)(2,1)} %bitcast.126, ...), custom_call_target="tpu_custom_call" | custom-call | flops 1409286144 | bytes 5505024 | tf_op jit(solution)/shard_map/pallas_call | solution.py:403
  213.6 4.2 %shard_map.465 = (bf16[2,224,768]{2,1,0:T(8,128)(2,1)}, bf16[2,224,768]{2,1,0:T(8,128)(2,1)}) custom-call(s32[3]{0:T(128)} %pad_add_fusion.refs_0_, bf16[4,2,224,256]{3,2,1,0:T(8,128)(2,1)} %bitcast.131, bf16[4,2,224,256]{3,2,1,0:T(8,128)(2,1)} %bitcast.32.refs_2_, bf16[4,2,224,256]{3,2,1,0:T(8,128)(2,1)} %bitcast.135, bf16[4,2,224,256]{3,2,1,0:T(8,128)(2,1)} %bitcast.137, ...), custom_call_target="tpu_custom_call" | custom-call | flops 704643072 | bytes 2752512 | tf_op jit(solution)/shard_map/pallas_call | solution.py:403
  217.8 1.5 collective-permute-start.23
  219.3 1.5 collective-permute-start.27
  220.9 4.8 %shard_map.468 = (bf16[1,224,1536]{2,1,0:T(8,128)(2,1)}, bf16[1,224,1536]{2,1,0:T(8,128)(2,1)}, bf16[1,224,1536]{2,1,0:T(8,128)(2,1)}, bf16[1,224,1536]{2,1,0:T(8,128)(2,1)}) custom-call(s32[4]{0:T(128)} %pad_add_fusion.1.refs_0_, bf16[1,2,1,224,1536]{4,3,2,1,0:T(8,128)(2,1)} %bitcast.147, bf16[1,2,1,224,1536]{4,3,2,1,0:T(8,128)(2,1)} %bitcast.52.refs_2_, ...), custom_call_target="tpu_custom_call" | custom-call | flops 8257536 | bytes 8257536 | tf_op jit(solution)/shard_map/pallas_call | solution.py:440
  227.6 2.1 fusion.12
  229.7 1.5 collective-permute-start.33
  232.4 4.2 %shard_map.464 = (bf16[2,224,768]{2,1,0:T(8,128)(2,1)}, bf16[2,224,768]{2,1,0:T(8,128)(2,1)}) custom-call(s32[3]{0:T(128)} %pad_add_fusion.2.refs_0_, bf16[4,2,224,256]{3,2,1,0:T(8,128)(2,1)} %bitcast.132, bf16[4,2,224,256]{3,2,1,0:T(8,128)(2,1)} %bitcast.32.refs_2_, bf16[4,2,224,256]{3,2,1,0:T(8,128)(2,1)} %bitcast.136, bf16[4,2,224,256]{3,2,1,0:T(8,128)(2,1)} %bitcast.138, ...), custom_call_target="tpu_custom_call" | custom-call | flops 704643072 | bytes 2752512 | tf_op jit(solution)/shard_map/pallas_call | solution.py:403
  237.9 6.5 %collective-permute-done.28 = bf16[2,224,768]{2,1,0:T(8,128)(2,1)} collective-permute-done((bf16[2,224,768]{2,1,0:T(8,128)(2,1)}, bf16[2,224,768]{2,1,0:T(8,128)(2,1)}, u32[]{:S(2)}, u32[]{:S(2)}) %collective-permute-start.28) | collective-permute-done | bytes 688160 | tf_op jit(solution)/shard_map/ppermute | solution.py:69
  244.4 3.1 %shard_map.466 = (bf16[1,224,768]{2,1,0:T(8,128)(2,1)}, bf16[1,224,768]{2,1,0:T(8,128)(2,1)}, bf16[1,224,768]{2,1,0:T(8,128)(2,1)}, bf16[1,224,768]{2,1,0:T(8,128)(2,1)}) custom-call(s32[4]{0:T(128)} %pad_add_fusion.1.refs_0_, bf16[1,2,1,224,768]{4,3,2,1,0:T(8,128)(2,1)} %bitcast.149, bf16[1,2,1,224,768]{4,3,2,1,0:T(8,128)(2,1)} %bitcast.36.refs_2_, ...), custom_call_target="tpu_custom_call" | custom-call | flops 4128768 | bytes 4128768 | tf_op jit(solution)/shard_map/pallas_call | solution.py:440
  248.5 2.9 %collective-permute-done.34 = bf16[1,224,1536]{2,1,0:T(8,128)(2,1)S(1)} collective-permute-done((bf16[1,224,1536]{2,1,0:T(8,128)(2,1)}, bf16[1,224,1536]{2,1,0:T(8,128)(2,1)S(1)}, u32[]{:S(2)}, u32[]{:S(2)}) %collective-permute-start.34) | collective-permute-done | bytes 688160 | tf_op jit(solution)/shard_map/ppermute | solution.py:69
  251.5 6.2 %collective-permute-done.33 = bf16[1,224,1536]{2,1,0:T(8,128)(2,1)} collective-permute-done((bf16[1,224,1536]{2,1,0:T(8,128)(2,1)}, bf16[1,224,1536]{2,1,0:T(8,128)(2,1)}, u32[]{:S(2)}, u32[]{:S(2)}) %collective-permute-start.33) | collective-permute-done | bytes 688160 | tf_op jit(solution)/shard_map/ppermute | solution.py:69
  257.6 6.0 %adv.1 = (f32[3584,128]{1,0:T(8,128)}, f32[3584,128]{1,0:T(8,128)}, f32[3584,128]{1,0:T(8,128)}, f32[3584,128]{1,0:T(8,128)}) custom-call(bf16[224,1536]{1,0:T(8,128)(2,1)} %bitcast.151, bf16[224,1536]{1,0:T(8,128)(2,1)} %bitcast.56.refs_1_, bf16[224,1536]{1,0:T(8,128)(2,1)} %bitcast.141, bf16[224,1536]{1,0:T(8,128)(2,1)} %bitcast.144, ...), custom_call_target="tpu_custom_call" | custom-call | flops 2293760 | bytes 14680064 | tf_op jit(solution)/shard_map/adv/pallas_call | solution.py:493
  263.6 3.3 %multiply_add_fusion = (f32[1024,224]{0,1:T(8,128)}, f32[1024,224]{0,1:T(8,128)}, f32[1024,224]{0,1:T(8,128)}) fusion(f32[1024,224]{0,1:T(8,128)} %param.47, f32[1024,224]{0,1:T(8,128)S(1)} %convert_element_type.103, f32[1024,224]{0,1:T(8,128)S(1)} %add_bitcast_fusion, f32[1024,224]{0,1:T(8,128)} %param.40), kind=kLoop, calls=%fused_computation.1 | loop fusion | flops 2293760 | bytes 6422528 | tf_op jit(solution)/shard_map/add | solution.py:33
  267.0 7.2 %last.1 = (f32[224,2,448]{2,1,0:T(2,128)}, f32[224,2,448]{2,1,0:T(2,128)}, f32[224,2,448]{2,1,0:T(2,128)}, f32[224,2,448]{2,1,0:T(2,128)}, f32[128,224]{1,0:T(8,...) custom-call(bf16[224,768]{1,0:T(8,128)(2,1)} %bitcast.153, ...), custom_call_target="tpu_custom_call" | custom-call | flops 3010560 | bytes 10035200 | tf_op jit(solution)/shard_map/last/pallas_call | solution.py:789
  (139 shorter events, 29.2 us)
Async XLA Ops:
  0.7 29.5 %copy-start.27 = (s32[256]{0:T(256)S(1)}, s32[256]{0:T(256)}, u32[]{:S(2)}) copy-start(s32[256]{0:T(256)} %param.26) | copy-start | bytes 3076
  27.8 35.3 %copy-start.13 = (bf16[448,256]{1,0:T(8,128)(2,1)}, bf16[448,256]{1,0:T(8,128)(2,1)S(1)}, u32[]{:S(2)}) copy-start(bf16[448,256]{1,0:T(8,128)(2,1)S(1)} %select_bitcast_fusion.rest_0_) | copy-start | bytes 688132
  27.8 60.8 %collective-permute-start.3 = (bf16[448,256]{1,0:T(8,128)(2,1)S(1)}, bf16[448,256]{1,0:T(8,128)(2,1)S(1)}, u32[]{:S(2)}, u32[]{:S(2)}) collective-permute-start(bf16[448,256]{1,0:T(8,128)(2,1)S(1)} %select_bitcast_fusion.rest_0_), channel_id=1, source_target_pairs={{0,1},{1,0},{2,3},{3,2},{4,5},{5,4},{6,7},{7,6},{8,9},{9,8},{10,11... | collective-permute-start | bytes 688136 | tf_op jit(solution)/shard_map/ppermute | solution.py:74
  27.9 60.7 %collective-permute-start.4 = (bf16[448,256]{1,0:T(8,128)(2,1)S(1)}, bf16[448,256]{1,0:T(8,128)(2,1)S(1)}, u32[]{:S(2)}, u32[]{:S(2)}) collective-permute-start(bf16[448,256]{1,0:T(8,128)(2,1)S(1)} %select_bitcast_fusion.rest_0_), channel_id=1, source_target_pairs={{0,2},{1,3},{2,0},{3,1},{4,6},{5,7},{6,4},{7,5},{8,10},{9,11},{10,... | collective-permute-start | bytes 688136 | tf_op jit(solution)/shard_map/ppermute | solution.py:74
  38.8 24.3 %collective-permute-start.2 = (bf16[448,256]{1,0:T(8,128)(2,1)}, bf16[448,256]{1,0:T(8,128)(2,1)S(1)}, u32[]{:S(2)}, u32[]{:S(2)}) collective-permute-start(bf16[448,256]{1,0:T(8,128)(2,1)} %get-tuple-element.111), channel_id=1, source_target_pairs={{0,3},{1,2},{2,1},{3,0},{4,7},{5,6},{6,5},{7,4},{8,11},{9,10},{10,... | collective-permute-start | bytes 688136 | tf_op jit(solution)/shard_map/ppermute | solution.py:74
  40.9 24.3 %collective-permute-start.1 = (bf16[448,256]{1,0:T(8,128)(2,1)}, bf16[448,256]{1,0:T(8,128)(2,1)S(1)}, u32[]{:S(2)}, u32[]{:S(2)}) collective-permute-start(bf16[448,256]{1,0:T(8,128)(2,1)} %get-tuple-element.110), channel_id=1, source_target_pairs={{0,2},{1,3},{2,0},{3,1},{4,6},{5,7},{6,4},{7,5},{8,10},{9,11},{10,... | collective-permute-start | bytes 688136 | tf_op jit(solution)/shard_map/ppermute | solution.py:74
  40.9 24.3 %collective-permute-start = (bf16[448,256]{1,0:T(8,128)(2,1)}, bf16[448,256]{1,0:T(8,128)(2,1)S(1)}, u32[]{:S(2)}, u32[]{:S(2)}) collective-permute-start(bf16[448,256]{1,0:T(8,128)(2,1)} %get-tuple-element.109), channel_id=1, source_target_pairs={{0,1},{1,0},{2,3},{3,2},{4,5},{5,4},{6,7},{7,6},{8,9},{9,8},{10,11... | collective-permute-start | bytes 688136 | tf_op jit(solution)/shard_map/ppermute | solution.py:74
  58.3 6.9 %copy-start.2 = (bf16[256,448]{0,1:T(8,128)(2,1)S(1)}, bf16[256,448]{0,1:T(8,128)(2,1)}, u32[]{:S(2)}) copy-start(bf16[256,448]{0,1:T(8,128)(2,1)} %param.24) | copy-start | bytes 688132
  58.3 6.9 %copy-start.7 = (f32[448,256]{1,0:T(8,128)S(1)}, f32[448,256]{1,0:T(8,128)}, u32[]{:S(2)}) copy-start(f32[448,256]{1,0:T(8,128)} %get-tuple-element.108) | copy-start | bytes 1376260
  63.1 25.5 %collective-permute-start.5 = (bf16[448,256]{1,0:T(8,128)(2,1)S(1)}, bf16[448,256]{1,0:T(8,128)(2,1)S(1)}, u32[]{:S(2)}, u32[]{:S(2)}) collective-permute-start(bf16[448,256]{1,0:T(8,128)(2,1)S(1)} %select_bitcast_fusion.rest_0_), channel_id=1, source_target_pairs={{0,3},{1,2},{2,1},{3,0},{4,7},{5,6},{6,5},{7,4},{8,11},{9,10},{10,... | collective-permute-start | bytes 688136 | tf_op jit(solution)/shard_map/ppermute | solution.py:74
  65.2 37.6 %copy-start.9 = (bf16[448,256]{1,0:T(8,128)(2,1)}, bf16[448,256]{1,0:T(8,128)(2,1)S(1)}, u32[]{:S(2)}) copy-start(bf16[448,256]{1,0:T(8,128)(2,1)S(1)} %collective-permute-done) | copy-start | bytes 688132
  102.8 9.6 %collective-permute-start.14 = (bf16[3,256,1024]{2,1,0:T(8,128)(2,1)}, bf16[3,256,1024]{2,1,0:T(8,128)(2,1)S(1)}, u32[]{:S(2)}, u32[]{:S(2)}) collective-permute-start(bf16[3,256,1024]{2,1,0:T(8,128)(2,1)} %get-tuple-element.114.act_ref.refs_5_), channel_id=1, source_target_pairs={{0,4},{4,0},{8,12},{12,8},{16,20},{20,16},{24,28},{28,24},{1,5},{5... | collective-permute-start | bytes 4718600 | tf_op jit(solution)/shard_map/ppermute | solution.py:69
  102.9 5.1 %collective-permute-start.12 = (bf16[1792,256]{1,0:T(8,128)(2,1)}, bf16[1792,256]{1,0:T(8,128)(2,1)}, u32[]{:S(2)}, u32[]{:S(2)}) collective-permute-start(bf16[1792,256]{1,0:T(8,128)(2,1)} %get-tuple-element.132), channel_id=1, source_target_pairs={{0,4},{4,0},{8,12},{12,8},{16,20},{20,16},{24,28},{28,24},{1,5},{5... | collective-permute-start | bytes 2752520 | tf_op jit(solution)/shard_map/ppermute | solution.py:69
  103.4 9.1 %collective-permute-start.13 = (bf16[1792,256]{1,0:T(8,128)(2,1)}, bf16[1792,256]{1,0:T(8,128)(2,1)}, u32[]{:S(2)}, u32[]{:S(2)}) collective-permute-start(bf16[1792,256]{1,0:T(8,128)(2,1)} %get-tuple-element.120.cot_ref), channel_id=1, source_target_pairs={{0,4},{4,0},{8,12},{12,8},{16,20},{20,16},{24,28},{28,24},{1,5},{5... | collective-permute-start | bytes 2752520 | tf_op jit(solution)/shard_map/ppermute | solution.py:69
  103.4 15.8 %collective-permute-start.9 = (bf16[448,256]{1,0:T(8,128)(2,1)}, bf16[448,256]{1,0:T(8,128)(2,1)S(1)}, u32[]{:S(2)}, u32[]{:S(2)}) collective-permute-start(bf16[448,256]{1,0:T(8,128)(2,1)} %get-tuple-element.129), channel_id=1, source_target_pairs={{0,1},{1,0},{2,3},{3,2},{4,5},{5,4},{6,7},{7,6},{8,9},{9,8},{10,11... | collective-permute-start | bytes 688136 | tf_op jit(solution)/shard_map/ppermute | solution.py:74
  105.2 19.6 %collective-permute-start.10 = (bf16[448,256]{1,0:T(8,128)(2,1)}, bf16[448,256]{1,0:T(8,128)(2,1)}, u32[]{:S(2)}, u32[]{:S(2)}) collective-permute-start(bf16[448,256]{1,0:T(8,128)(2,1)} %get-tuple-element.130), channel_id=1, source_target_pairs={{0,2},{1,3},{2,0},{3,1},{4,6},{5,7},{6,4},{7,5},{8,10},{9,11},{10,... | collective-permute-start | bytes 688136 | tf_op jit(solution)/shard_map/ppermute | solution.py:74
  107.9 16.8 %collective-permute-start.11 = (bf16[448,256]{1,0:T(8,128)(2,1)}, bf16[448,256]{1,0:T(8,128)(2,1)}, u32[]{:S(2)}, u32[]{:S(2)}) collective-permute-start(bf16[448,256]{1,0:T(8,128)(2,1)} %get-tuple-element.131), channel_id=1, source_target_pairs={{0,3},{1,2},{2,1},{3,0},{4,7},{5,6},{6,5},{7,4},{8,11},{9,10},{10,... | collective-permute-start | bytes 688136 | tf_op jit(solution)/shard_map/ppermute | solution.py:74
  124.8 9.3 %copy-start.3 = (bf16[1792,256]{1,0:T(8,128)(2,1)S(1)}, bf16[1792,256]{1,0:T(8,128)(2,1)}, u32[]{:S(2)}) copy-start(bf16[1792,256]{1,0:T(8,128)(2,1)} %get-tuple-element.144) | copy-start | bytes 2752516
  127.1 14.0 %collective-permute-start.15 = (bf16[448,256]{1,0:T(8,128)(2,1)}, bf16[448,256]{1,0:T(8,128)(2,1)S(1)}, u32[]{:S(2)}, u32[]{:S(2)}) collective-permute-start(bf16[448,256]{1,0:T(8,128)(2,1)} %get-tuple-element.135.rest_0_), channel_id=1, source_target_pairs={{0,1},{1,0},{2,3},{3,2},{4,5},{5,4},{6,7},{7,6},{8,9},{9,8},{10,11... | collective-permute-start | bytes 688136 | tf_op jit(solution)/shard_map/ppermute | solution.py:74
  131.7 19.4 %collective-permute-start.16 = (bf16[448,256]{1,0:T(8,128)(2,1)}, bf16[448,256]{1,0:T(8,128)(2,1)S(1)}, u32[]{:S(2)}, u32[]{:S(2)}) collective-permute-start(bf16[448,256]{1,0:T(8,128)(2,1)} %get-tuple-element.135.rest_0_), channel_id=1, source_target_pairs={{0,2},{1,3},{2,0},{3,1},{4,6},{5,7},{6,4},{7,5},{8,10},{9,11},{10,... | collective-permute-start | bytes 688136 | tf_op jit(solution)/shard_map/ppermute | solution.py:74
  132.6 18.5 %collective-permute-start.17 = (bf16[448,256]{1,0:T(8,128)(2,1)}, bf16[448,256]{1,0:T(8,128)(2,1)S(1)}, u32[]{:S(2)}, u32[]{:S(2)}) collective-permute-start(bf16[448,256]{1,0:T(8,128)(2,1)} %get-tuple-element.135.rest_0_), channel_id=1, source_target_pairs={{0,3},{1,2},{2,1},{3,0},{4,7},{5,6},{6,5},{7,4},{8,11},{9,10},{10,... | collective-permute-start | bytes 688136 | tf_op jit(solution)/shard_map/ppermute | solution.py:74
  134.1 59.1 %collective-permute-start.24 = (bf16[1792,256]{1,0:T(8,128)(2,1)S(1)}, bf16[1792,256]{1,0:T(8,128)(2,1)}, u32[]{:S(2)}, u32[]{:S(2)}) collective-permute-start(bf16[1792,256]{1,0:T(8,128)(2,1)S(1)} %copy-done.3), channel_id=1, source_target_pairs={{0,4},{4,0},{8,12},{12,8},{16,20},{20,16},{24,28},{28,24},{1,5},{5... | collective-permute-start | bytes 2752520 | tf_op jit(solution)/shard_map/ppermute | solution.py:69
  141.0 10.9 %copy-start.16 = (bf16[448,256]{1,0:T(8,128)(2,1)}, bf16[448,256]{1,0:T(8,128)(2,1)S(1)}, u32[]{:S(2)}) copy-start(bf16[448,256]{1,0:T(8,128)(2,1)S(1)} %collective-permute-done.15.rest_1_) | copy-start | bytes 688132
  151.9 18.6 %copy-start.22 = (bf16[2,448]{1,0:T(2,128)(2,1)S(1)}, bf16[2,448]{1,0:T(2,128)(2,1)}, u32[]{:S(2)}) copy-start(bf16[2,448]{1,0:T(2,128)(2,1)} %param.27) | copy-start | bytes 5380
  151.9 21.6 %copy-start.11 = (f32[448,256]{1,0:T(8,128)S(1)}, f32[448,256]{1,0:T(8,128)}, u32[]{:S(2)}) copy-start(f32[448,256]{1,0:T(8,128)} %get-tuple-element.142) | copy-start | bytes 1376260
  165.2 10.2 %collective-permute-start.20 = (bf16[464,256]{1,0:T(8,128)(2,1)}, bf16[464,256]{1,0:T(8,128)(2,1)S(1)}, u32[]{:S(2)}, u32[]{:S(2)}) collective-permute-start(bf16[464,256]{1,0:T(8,128)(2,1)} %get-tuple-element.140), channel_id=1, source_target_pairs={{0,3},{1,2},{2,1},{3,0},{4,7},{5,6},{6,5},{7,4},{8,11},{9,10},{10,... | collective-permute-start | bytes 712712 | tf_op jit(solution)/shard_map/ppermute | solution.py:74
  167.6 19.8 %collective-permute-start.19 = (bf16[464,256]{1,0:T(8,128)(2,1)}, bf16[464,256]{1,0:T(8,128)(2,1)}, u32[]{:S(2)}, u32[]{:S(2)}) collective-permute-start(bf16[464,256]{1,0:T(8,128)(2,1)} %get-tuple-element.139), channel_id=1, source_target_pairs={{0,2},{1,3},{2,0},{3,1},{4,6},{5,7},{6,4},{7,5},{8,10},{9,11},{10,... | collective-permute-start | bytes 712712 | tf_op jit(solution)/shard_map/ppermute | solution.py:74
  170.3 17.2 %collective-permute-start.18 = (bf16[464,256]{1,0:T(8,128)(2,1)}, bf16[464,256]{1,0:T(8,128)(2,1)}, u32[]{:S(2)}, u32[]{:S(2)}) collective-permute-start(bf16[464,256]{1,0:T(8,128)(2,1)} %get-tuple-element.138), channel_id=1, source_target_pairs={{0,1},{1,0},{2,3},{3,2},{4,5},{5,4},{6,7},{7,6},{8,9},{9,8},{10,11... | collective-permute-start | bytes 712712 | tf_op jit(solution)/shard_map/ppermute | solution.py:74
  172.0 45.7 %collective-permute-start.31 = (bf16[2,224,1536]{2,1,0:T(8,128)(2,1)}, bf16[2,224,1536]{2,1,0:T(8,128)(2,1)}, u32[]{:S(2)}, u32[]{:S(2)}) collective-permute-start(bf16[2,224,1536]{2,1,0:T(8,128)(2,1)} %get-tuple-element.133.refs_4_), channel_id=1, source_target_pairs={{0,8},{4,12},{8,0},{12,4},{16,24},{20,28},{24,16},{28,20},{1,9},{5... | collective-permute-start | bytes 4128776 | tf_op jit(solution)/shard_map/ppermute | solution.py:69
  175.4 12.1 %copy-start.20 = (bf16[464,256]{1,0:T(8,128)(2,1)}, bf16[464,256]{1,0:T(8,128)(2,1)S(1)}, u32[]{:S(2)}) copy-start(bf16[464,256]{1,0:T(8,128)(2,1)S(1)} %collective-permute-done.20) | copy-start | bytes 712708
  175.4 44.0 %collective-permute-start.32 = (bf16[2,224,1536]{2,1,0:T(8,128)(2,1)}, bf16[2,224,1536]{2,1,0:T(8,128)(2,1)}, u32[]{:S(2)}, u32[]{:S(2)}) collective-permute-start(bf16[2,224,1536]{2,1,0:T(8,128)(2,1)} %get-tuple-element.134.refs_5_), channel_id=1, source_target_pairs={{0,16},{4,20},{8,24},{12,28},{16,0},{20,4},{24,8},{28,12},{1,17},{... | collective-permute-start | bytes 4128776 | tf_op jit(solution)/shard_map/ppermute | solution.py:69
  187.5 18.2 %collective-permute-start.25 = (bf16[1792,256]{1,0:T(8,128)(2,1)}, bf16[1792,256]{1,0:T(8,128)(2,1)S(1)}, u32[]{:S(2)}, u32[]{:S(2)}) collective-permute-start(bf16[1792,256]{1,0:T(8,128)(2,1)} %get-tuple-element.145), channel_id=1, source_target_pairs={{0,4},{4,0},{8,12},{12,8},{16,20},{20,16},{24,28},{28,24},{1,5},{5... | collective-permute-start | bytes 2752520 | tf_op jit(solution)/shard_map/ppermute | solution.py:69
  190.8 1.4 collective-permute-start.21
  192.2 12.8 %collective-permute-start.26 = (bf16[1,256,1536]{2,1,0:T(8,128)(2,1)}, bf16[1,256,1536]{2,1,0:T(8,128)(2,1)}, u32[]{:S(2)}, u32[]{:S(2)}) collective-permute-start(bf16[1,256,1536]{2,1,0:T(8,128)(2,1)} %get-tuple-element.146.refs_5_), channel_id=1, source_target_pairs={{0,4},{4,0},{8,12},{12,8},{16,20},{20,16},{24,28},{28,24},{1,5},{5... | collective-permute-start | bytes 2359304 | tf_op jit(solution)/shard_map/ppermute | solution.py:69
  193.2 9.4 %collective-permute-start.22 = (f32[8,448]{1,0:T(8,128)S(1)}, f32[8,448]{1,0:T(8,128)S(1)}, u32[]{:S(2)}, u32[]{:S(2)}) collective-permute-start(f32[8,448]{1,0:T(8,128)S(1)} %fusion.23), channel_id=1, source_target_pairs={{0,8},{4,12},{8,0},{12,4},{16,24},{20,28},{24,16},{28,20},{1,9},{5... | collective-permute-start | bytes 43016 | tf_op jit(solution)/shard_map/ppermute | solution.py:69
  202.6 23.1 %collective-permute-start.8 = (bf16[448,256]{1,0:T(8,128)(2,1)}, bf16[448,256]{1,0:T(8,128)(2,1)S(1)}, u32[]{:S(2)}, u32[]{:S(2)}) collective-permute-start(bf16[448,256]{1,0:T(8,128)(2,1)} %get-tuple-element.118), channel_id=1, source_target_pairs={{0,3},{1,2},{2,1},{3,0},{4,7},{5,6},{6,5},{7,4},{8,11},{9,10},{10,... | collective-permute-start | bytes 688136 | tf_op jit(solution)/shard_map/ppermute | solution.py:74
  205.0 21.3 %collective-permute-start.7 = (bf16[448,256]{1,0:T(8,128)(2,1)}, bf16[448,256]{1,0:T(8,128)(2,1)S(1)}, u32[]{:S(2)}, u32[]{:S(2)}) collective-permute-start(bf16[448,256]{1,0:T(8,128)(2,1)} %get-tuple-element.117), channel_id=1, source_target_pairs={{0,2},{1,3},{2,0},{3,1},{4,6},{5,7},{6,4},{7,5},{8,10},{9,11},{10,... | collective-permute-start | bytes 688136 | tf_op jit(solution)/shard_map/ppermute | solution.py:74
  205.6 7.9 %copy-start.4 = (bf16[1792,256]{1,0:T(8,128)(2,1)}, bf16[1792,256]{1,0:T(8,128)(2,1)S(1)}, u32[]{:S(2)}) copy-start(bf16[1792,256]{1,0:T(8,128)(2,1)S(1)} %collective-permute-done.25) | copy-start | bytes 2752516
  205.6 22.0 %collective-permute-start.6 = (bf16[448,256]{1,0:T(8,128)(2,1)}, bf16[448,256]{1,0:T(8,128)(2,1)}, u32[]{:S(2)}, u32[]{:S(2)}) collective-permute-start(bf16[448,256]{1,0:T(8,128)(2,1)} %get-tuple-element.116), channel_id=1, source_target_pairs={{0,1},{1,0},{2,3},{3,2},{4,5},{5,4},{6,7},{7,6},{8,9},{9,8},{10,11... | collective-permute-start | bytes 688136 | tf_op jit(solution)/shard_map/ppermute | solution.py:74
  217.8 11.9 %collective-permute-start.23 = (f32[8,448]{1,0:T(8,128)S(1)}, f32[8,448]{1,0:T(8,128)S(1)}, u32[]{:S(2)}, u32[]{:S(2)}) collective-permute-start(f32[8,448]{1,0:T(8,128)S(1)} %add.146), channel_id=1, source_target_pairs={{0,16},{4,20},{8,24},{12,28},{16,0},{20,4},{24,8},{28,12},{1,17},{... | collective-permute-start | bytes 43016 | tf_op jit(solution)/shard_map/ppermute | solution.py:69
  219.3 18.6 %collective-permute-start.27 = (bf16[2,224,768]{2,1,0:T(8,128)(2,1)}, bf16[2,224,768]{2,1,0:T(8,128)(2,1)}, u32[]{:S(2)}, u32[]{:S(2)}) collective-permute-start(bf16[2,224,768]{2,1,0:T(8,128)(2,1)} %get-tuple-element.148), channel_id=1, source_target_pairs={{0,8},{4,12},{8,0},{12,4},{16,24},{20,28},{24,16},{28,20},{1,9},{5... | collective-permute-start | bytes 2064392 | tf_op jit(solution)/shard_map/ppermute | solution.py:69
  225.7 18.7 %collective-permute-start.28 = (bf16[2,224,768]{2,1,0:T(8,128)(2,1)}, bf16[2,224,768]{2,1,0:T(8,128)(2,1)}, u32[]{:S(2)}, u32[]{:S(2)}) collective-permute-start(bf16[2,224,768]{2,1,0:T(8,128)(2,1)} %get-tuple-element.150), channel_id=1, source_target_pairs={{0,16},{4,20},{8,24},{12,28},{16,0},{20,4},{24,8},{28,12},{1,17},{... | collective-permute-start | bytes 2064392 | tf_op jit(solution)/shard_map/ppermute | solution.py:69
  227.1 24.3 %collective-permute-start.34 = (bf16[1,224,1536]{2,1,0:T(8,128)(2,1)}, bf16[1,224,1536]{2,1,0:T(8,128)(2,1)S(1)}, u32[]{:S(2)}, u32[]{:S(2)}) collective-permute-start(bf16[1,224,1536]{2,1,0:T(8,128)(2,1)} %get-tuple-element.166), channel_id=1, source_target_pairs={{0,8},{4,12},{8,0},{12,4},{16,24},{20,28},{24,16},{28,20},{1,9},{5... | collective-permute-start | bytes 2064392 | tf_op jit(solution)/shard_map/ppermute | solution.py:69
  229.7 28.0 %collective-permute-start.33 = (bf16[1,224,1536]{2,1,0:T(8,128)(2,1)}, bf16[1,224,1536]{2,1,0:T(8,128)(2,1)}, u32[]{:S(2)}, u32[]{:S(2)}) collective-permute-start(bf16[1,224,1536]{2,1,0:T(8,128)(2,1)} %get-tuple-element.164), channel_id=1, source_target_pairs={{0,16},{4,20},{8,24},{12,28},{16,0},{20,4},{24,8},{28,12},{1,17},{... | collective-permute-start | bytes 2064392 | tf_op jit(solution)/shard_map/ppermute | solution.py:69
  236.6 14.7 %copy-start.5 = (bf16[1,224,1536]{2,1,0:T(8,128)(2,1)S(1)}, bf16[1,224,1536]{2,1,0:T(8,128)(2,1)}, u32[]{:S(2)}) copy-start(bf16[1,224,1536]{2,1,0:T(8,128)(2,1)} %get-tuple-element.165) | copy-start | bytes 2064388
  247.5 19.5 %collective-permute-start.29 = (bf16[1,224,768]{2,1,0:T(8,128)(2,1)}, bf16[1,224,768]{2,1,0:T(8,128)(2,1)}, u32[]{:S(2)}, u32[]{:S(2)}) collective-permute-start(bf16[1,224,768]{2,1,0:T(8,128)(2,1)} %get-tuple-element.152), channel_id=1, source_target_pairs={{0,16},{4,20},{8,24},{12,28},{16,0},{20,4},{24,8},{28,12},{1,17},{... | collective-permute-start | bytes 1032200 | tf_op jit(solution)/shard_map/ppermute | solution.py:69
  247.9 19.0 %collective-permute-start.30 = (bf16[1,224,768]{2,1,0:T(8,128)(2,1)}, bf16[1,224,768]{2,1,0:T(8,128)(2,1)}, u32[]{:S(2)}, u32[]{:S(2)}) collective-permute-start(bf16[1,224,768]{2,1,0:T(8,128)(2,1)} %get-tuple-element.154), channel_id=1, source_target_pairs={{0,8},{4,12},{8,0},{12,4},{16,24},{20,28},{24,16},{28,20},{1,9},{5... | collective-permute-start | bytes 1032200 | tf_op jit(solution)/shard_map/ppermute | solution.py:69
  251.5 12.2 %copy-start.1 = (f32[1024,224]{0,1:T(8,128)}, f32[1024,224]{0,1:T(8,128)S(1)}, u32[]{:S(2)}) copy-start(f32[1024,224]{0,1:T(8,128)S(1)} %add_bitcast_fusion) | copy-start | bytes 2752516
  (18 other events, 67.7 us)
where the time goes:
time: 275 us; the launch traced here: 274 us
  Pallas kernels  82.5 us (30%)
  waiting for transfers between devices  54.3 us (20%)
  blocking collectives  46.8 us (17%)
  starting transfers between devices  46.5 us (17%)
  other arithmetic  24.7 us (9%)
  local copies, waits for them, and re-layouts  18.4 us (7%)
    ppermute x18, starting transfers between devices, swap_tensor(): lax.ppermute(source, TENSOR, [(k, k ^ distance) for k in range(count)])  33.9 us
    ppermute x18, waiting for transfers between devices, swap_tensor(): lax.ppermute(source, TENSOR, [(k, k ^ distance) for k in range(count)])  33.1 us
    all_gather x1, blocking collectives, local(): packed_whole = lax.all_gather(packed, TENSOR)  23.5 us
    all_gather x1, blocking collectives, local(): hidden = lax.all_gather(hidden_own.astype(BF), TENSOR, axis=0, tiled=True)  23.3 us
    ppermute x17, waiting for transfers between devices, swap_dp(): return lax.ppermute(source, DP, [(k, k ^ 1 << bit) for k in range(count)])  21.2 us
    pallas_call x4, Pallas kernels, sum_rows(): pl.pallas_call(lambda *refs: stage_kernel(orders, tile, *refs), out_shape...  20.1 us
    pallas_call x1, Pallas kernels, local(): pl.pallas_call(ffn_kernel, out_shape=[shaped(width, tokens, dtype=BF), sh...  13.3 us
    pallas_call x1, Pallas kernels, local(): pl.pallas_call(back_kernel, out_shape=[shaped(share, tokens), shaped(widt...  13.3 us
  transfers between devices with their start and end apart: 35, of which 11 were waited for; matrix products, arithmetic and copies ran while one was open for 13% of the time, Pallas kernels for 22%

commit v1 on v0

--- a/solution.py
+++ b/solution.py
@@ -76,7 +76,8 @@
 
 def sum_dp(source):
     for bit in range(lax.axis_size(DP).bit_length() - 1):
-        source = source + swap_dp(source, bit)
+        arrived = swap_dp(source, bit)
+        source = source + arrived
     return source
 
 
@@ -161,7 +162,7 @@
         feats = slice(h * F, (h + 1) * F)
         vals = slice(h * size, (h + 1) * size)
         _, weights, totals = weigh(qk_ref[0, :, feats], qk_ref[1, :, feats], allowed)
-        attended_ref[:, vals] = dot((weights / totals).astype(BF), mixed_ref[:, vals])
+        attended_ref[:, vals] = dot((weights * (1.0 / totals)).astype(BF), mixed_ref[:, vals])
     gates = vg_ref[1]
     gated = (attended_ref[...] * (gates * jax.nn.sigmoid(gates))).astype(BF)
     gated_ref[...] = gated
@@ -178,47 +179,39 @@
     cot_pieces, rest = rest[:count], rest[count:]
     cot_ref, turned_ref, root_ref, right_ref, keep_ref = rest[:5]
     send_refs, (normed_ref, wide_ref) = rest[5:-2], rest[-2:]
-    step = pl.program_id(0)
-
-    @pl.when(step == 0)
-    def _():
-        place_rows(own_ref[0], cot_ref, cot_pieces)
-        total = jnp.zeros((1, tokens), F32)
-        for start in range(0, width, 256):
-            block = hidden_ref[start : start + 256, :].astype(F32)
-            total = total + jnp.sum(block * block, axis=0, keepdims=True)
-        root = lax.rsqrt(total / width + epsilon)
-        root_ref[...] = jnp.broadcast_to(root, root_ref.shape)
-        for start in range(0, width, 256):
-            piece = (
-                hidden_ref[start : start + 256, :].astype(F32)
-                * root
-                * gain_ref[start : start + 256, 1:2]
-            )
-            turned_ref[start : start + 256, :] = piece.astype(BF)
-            normed_ref[:, start : start + 256] = piece.T.astype(BF)
-            wide_ref[start : start + 256, :] = jnp.zeros((256, tokens), F32)
-
-    normed = normed_ref[...]
-    gate = dot(normed, gate_up_ref[0])
-    up = dot(normed, gate_up_ref[1])
-    d_act = dot(down_ref[...], cot_ref[...]).T
-    logistic = jax.nn.sigmoid(gate)
-    silu = gate * logistic
-    right_ref[0] = (d_act * up * slope_of(gate, logistic)).astype(BF)
-    right_ref[1] = (d_act * silu).astype(BF)
-    right_ref[2] = (silu * up).astype(BF)
+    tile = 512
+    place_rows(own_ref[0], cot_ref, cot_pieces)
+    total = jnp.zeros((1, tokens), F32)
+    for start in range(0, width, 256):
+        block = hidden_ref[start : start + 256, :].astype(F32)
+        total = total + jnp.sum(block * block, axis=0, keepdims=True)
+    root = lax.rsqrt(total / width + epsilon)
+    root_ref[...] = jnp.broadcast_to(root, root_ref.shape)
     for start in range(0, width, 256):
         rows = slice(start, start + 256)
-        wide_ref[rows, :] = (
-            wide_ref[rows, :]
-            + dot(gate_up_ref[0, rows, :], right_ref[0], 1, 1)
-            + dot(gate_up_ref[1, rows, :], right_ref[1], 1, 1)
+        piece = hidden_ref[rows, :].astype(F32) * root * gain_ref[rows, 1:2]
+        turned_ref[rows, :] = piece.astype(BF)
+        normed_ref[:, rows] = piece.T.astype(BF)
+        wide_ref[rows, :] = jnp.zeros((256, tokens), F32)
+
+    @pl.loop(0, down_ref.shape[0] // tile)
+    def _(step):
+        units = pl.ds(pl.multiple_of(step * tile, tile), tile)
+        gate = dot(normed_ref[...], gate_up_ref[0, :, units])
+        up = dot(normed_ref[...], gate_up_ref[1, :, units])
+        d_act = dot(down_ref[units, :], cot_ref[...]).T
+        logistic = jax.nn.sigmoid(gate)
+        silu = gate * logistic
+        right_ref[0, :, units] = (d_act * up * slope_of(gate, logistic)).astype(BF)
+        right_ref[1, :, units] = (d_act * silu).astype(BF)
+        right_ref[2, :, units] = (silu * up).astype(BF)
+        wide_ref[...] = (
+            wide_ref[...]
+            + dot(gate_up_ref[0, :, units], right_ref[0, :, units], 1, 1)
+            + dot(gate_up_ref[1, :, units], right_ref[1, :, units], 1, 1)
         )
 
-    @pl.when(step == pl.num_programs(0) - 1)
-    def _():
-        send_blocks(own_ref[0], wide_ref, keep_ref, send_refs)
+    send_blocks(own_ref[0], wide_ref, keep_ref, send_refs)
 
 
 def feed_kernel(own_ref, act_ref, down_ref, keep_ref, *rest):
@@ -288,11 +281,12 @@
         vals = slice(h * size, (h + 1) * size)
         queries, keys = qk_ref[0, :, feats], qk_ref[1, :, feats]
         scores, weights, totals = weigh(queries, keys, allowed)
-        probs = weights / totals
+        inverse = 1.0 / totals
+        probs = weights * inverse
         d_att = shift_ref[8 : 8 + tokens, vals].astype(BF)
         d_mixed_ref[:, vals] = dot(probs.T.astype(BF), d_att)
         d_probs = dot(d_att, mixed_ref[:, vals], 1, 1)
-        d_weights = (d_probs - jnp.sum(d_probs * probs, axis=1, keepdims=True)) / totals
+        d_weights = (d_probs - jnp.sum(d_probs * probs, axis=1, keepdims=True)) * inverse
         d_scores = jnp.where(allowed, d_weights * (1.0 + scores), 0.0)
         d_q = dot(d_scores.astype(BF), keys) * SCALE
         d_k = dot(d_scores.T.astype(BF), queries) * SCALE
@@ -572,14 +566,15 @@
     packed = jnp.concatenate(
         [inputs_turned, jnp.pad(gain_lines, ((0, EXTRA - 2 * pieces), (0, 0)))], axis=0
     )
+    documents_column = documents[:, None]
+    masked = jnp.where(documents_column >= 0, cotangent, jnp.zeros_like(cotangent)).T
+    masked, packed = lax.optimization_barrier((masked, packed))
     packed_whole = lax.all_gather(packed, TENSOR)
-    documents_column = documents[:, None]
     lines = [documents.astype(F32)]
     for offset in range(1, KERNEL):
         earlier = jnp.pad(documents, (offset, 0), constant_values=-2)[:tokens]
         lines.append((earlier == documents).astype(F32))
     lines = jnp.pad(jnp.stack(lines), ((0, 8 - KERNEL), (0, 0)))
-    masked = jnp.where(documents_column >= 0, cotangent, jnp.zeros_like(cotangent)).T
     masked, packed_whole = lax.optimization_barrier((masked, packed_whole))
 
     def sends(extra=0):
@@ -644,7 +639,6 @@
         hidden_own = hidden_own + piece.astype(F32)
     hidden = lax.all_gather(hidden_own.astype(BF), TENSOR, axis=0, tiled=True)
 
-    tile = 256
     cot_turned, normed_two_turned, root_two, ffn_right, keep_two, *sends_two = pl.pallas_call(
         ffn_kernel,
         out_shape=[
@@ -655,23 +649,7 @@
             shaped(share, tokens),
         ]
         + sends(),
-        grid=(hidden_units // tile,),
-        in_specs=[
-            scalars(),
-            pl.BlockSpec((width, tokens), lambda f: (0, 0)),
-            pl.BlockSpec((width, 2), lambda f: (0, 0)),
-            pl.BlockSpec((2, width, tile), lambda f: (0, 0, f)),
-            pl.BlockSpec((tile, width), lambda f: (f, 0)),
-        ]
-        + [pl.BlockSpec((share, tokens), lambda f: (0, 0))] * groups,
-        out_specs=[
-            pl.BlockSpec((width, tokens), lambda f: (0, 0)),
-            pl.BlockSpec((width, tokens), lambda f: (0, 0)),
-            pl.BlockSpec((8, tokens), lambda f: (0, 0)),
-            pl.BlockSpec((3, tokens, tile), lambda f: (0, 0, f)),
-            pl.BlockSpec((share, tokens), lambda f: (0, 0)),
-        ]
-        + [pl.BlockSpec((share, tokens), lambda f: (0, 0)) for _ in range(groups - 1)],
+        in_specs=[scalars()] + [vmem] * (4 + groups),
         scratch_shapes=[pltpu.VMEM((tokens, width), BF), pltpu.VMEM((width, tokens), F32)],
         cost_estimate=cost(10 * tokens * width * hidden_units, 6 * width * hidden_units),
         name="ffn",

time: 275 us -> 276 us (level)
  transfers between devices with their start and end apart: 35 -> 35, of which waited for: 11 -> 10; matrix products, arithmetic and copies ran while one was open for 13% -> 13% of each run, Pallas kernels for 22% -> 22%
where the time goes in v1:
time: 276 us; the launch traced here: 275 us
  Pallas kernels  83.5 us (30%)
  waiting for transfers between devices  53.9 us (20%)
  starting transfers between devices  46.9 us (17%)
  blocking collectives  46.8 us (17%)
  other arithmetic  24.8 us (9%)
  local copies, waits for them, and re-layouts  18.2 us (7%)
    ppermute x18, starting transfers between devices, swap_tensor(): lax.ppermute(source, TENSOR, [(k, k ^ distance) for k in range(count)])  34.2 us
    ppermute x18, waiting for transfers between devices, swap_tensor(): lax.ppermute(source, TENSOR, [(k, k ^ distance) for k in range(count)])  33.4 us
    all_gather x1, blocking collectives, local(): packed_whole = lax.all_gather(packed, TENSOR)  23.6 us
    all_gather x1, blocking collectives, local(): hidden = lax.all_gather(hidden_own.astype(BF), TENSOR, axis=0, tiled=True)  23.2 us
    ppermute x17, waiting for transfers between devices, swap_dp(): return lax.ppermute(source, DP, [(k, k ^ 1 << bit) for k in range(count)])  20.5 us
    pallas_call x4, Pallas kernels, sum_rows(): pl.pallas_call(lambda *refs: stage_kernel(orders, tile, *refs), out_shape...  20.1 us
    pallas_call x1, Pallas kernels, local(): pl.pallas_call(ffn_kernel, out_shape=[shaped(width, tokens, dtype=BF), sh...  14.3 us
    pallas_call x1, Pallas kernels, local(): pl.pallas_call(back_kernel, out_shape=[shaped(share, tokens), shaped(widt...  13.3 us
  transfers between devices with their start and end apart: 35, of which 10 were waited for; matrix products, arithmetic and copies ran while one was open for 13% of the time, Pallas kernels for 22%

profile of v1, /device:TPU:0, one launch (start us, length us, event | category | flops | bytes accessed | tf_op | source)
XLA Modules:
  0.0 275.1 jit_solution(4915601073442762299)
XLA Ops:
  4.3 23.6 %all-gather = bf16[1856,256]{1,0:T(8,128)(2,1)} all-gather(bf16[464,256]{1,0:T(8,128)(2,1)S(1)} %fusion.11), channel_id=2, replica_groups=mesh['dp'=8,'tensor'=4] {'tensor'}, dimensions={0}, use_global_device_ids=true | all-gather | bytes 1187840 | tf_op jit(solution)/shard_map/all_gather | solution.py:572
  28.0 2.3 collective-permute-start.4
  30.8 8.0 %head.1 = (bf16[1792,256]{1,0:T(8,128)(2,1)}, bf16[1792,256]{1,0:T(8,128)(2,1)}, f32[8,256]{1,0:T(8,128)}, f32[1792,2]{1,0:T(8,128)}, bf16[2,256,64]{2,1,0:T(8,1...) custom-call(s32[1]{0:T(128)} %bitcast.1.own_ref, ...), custom_call_target="tpu_custom_call" | custom-call | flops 1438646272 | bytes 8028160 | tf_op jit(solution)/shard_map/head/pallas_call | solution.py:590
  38.9 2.1 collective-permute-start.2
  41.0 2.2 collective-permute-start
  44.5 1.9 dynamic-slice_convert_fusion.1.refs_10_
  48.3 1.4 constant_dynamic-slice_fusion
  50.0 8.3 %copy.68 = bf16[1792,2,1024]{2,0,1:T(8,128)(2,1)} copy(bf16[1792,2,1024]{2,1,0:T(2,128)(2,1)} %param.32) | data formatting | bytes 14680064 | tf_op args[8]
  58.3 1.7 dynamic-slice_convert_fusion.2
  60.0 3.1 %dynamic-slice_convert_fusion = f32[224,2,1024]{2,1,0:T(2,128)} fusion(bf16[1792,2,1024]{2,1,0:T(2,128)(2,1)} %param.32, s32[]{:T(128)S(6)} %select_n.14), kind=kLoop, calls=%fused_computation.5 | loop fusion | flops 458752 | bytes 2752516 | tf_op jit(solution)/shard_map/convert_element_type | solution.py:632
  63.1 2.1 collective-permute-start.5
  65.4 23.2 %all_gather.11.hidden_ref = bf16[1792,256]{1,0:T(8,128)(2,1)} all-gather(bf16[448,256]{1,0:T(8,128)(2,1)S(1)} %fusion.24), channel_id=1, replica_groups=mesh['dp'=8,'tensor'=4] {'tensor'}, dimensions={0}, use_global_device_ids=true | all-gather | bytes 1146880 | tf_op jit(solution)/shard_map/all_gather | solution.py:640
  89.5 14.3 %ffn.1 = (bf16[1792,256]{1,0:T(8,128)(2,1)}, bf16[1792,256]{1,0:T(8,128)(2,1)}, f32[8,256]{1,0:T(8,128)}, bf16[3,256,1024]{2,1,0:T(8,128)(2,1)}, f32[448,256]{1,...) custom-call(s32[1]{0:T(128)} %bitcast.1.own_ref, ...), custom_call_target="tpu_custom_call" | custom-call | flops 4697620480 | bytes 11010048 | tf_op jit(solution)/shard_map/ffn/pallas_call | solution.py:642
  104.4 2.1 collective-permute-start.9
  106.5 2.7 collective-permute-start.10
  109.1 3.9 %collective-permute-start.11 = (bf16[448,256]{1,0:T(8,128)(2,1)}, bf16[448,256]{1,0:T(8,128)(2,1)}, u32[]{:S(2)}, u32[]{:S(2)}) collective-permute-start(bf16[448,256]{1,0:T(8,128)(2,1)} %get-tuple-element.135), channel_id=1, source_target_pairs={{0,3},{1,2},{2,1},{3,0},{4,7},{5,6},{6,5},{7,4},{8,11},{9,10},{10,... | collective-permute-start | bytes 688136 | tf_op jit(solution)/shard_map/ppermute | solution.py:74
  114.9 5.7 %shard_map.463 = (bf16[2,224,1536]{2,1,0:T(8,128)(2,1)}, bf16[2,224,1536]{2,1,0:T(8,128)(2,1)}) custom-call(s32[3]{0:T(128)} %pad_add_fusion.refs_0_, bf16[4,2,224,256]{3,2,1,0:T(8,128)(2,1)} %bitcast.133, bf16[4,2,224,256]{3,2,1,0:T(8,128)(2,1)} %bitcast.18.refs_2_, bf16[4,2,224,256]{3,2,1,0:T(8,128)(2,1)} %bitcast.125, ...), custom_call_target="tpu_custom_call" | custom-call | flops 1409286144 | bytes 5505024 | tf_op jit(solution)/shard_map/pallas_call | solution.py:397
  120.6 5.5 %collective-permute-done.10.refs_2_ = bf16[448,256]{1,0:T(8,128)(2,1)} collective-permute-done((bf16[448,256]{1,0:T(8,128)(2,1)}, bf16[448,256]{1,0:T(8,128)(2,1)}, u32[]{:S(2)}, u32[]{:S(2)}) %collective-permute-start.10) | collective-permute-done | bytes 229408 | tf_op jit(solution)/shard_map/ppermute | solution.py:74
  126.1 2.3 add.295
  128.3 4.7 %collective-permute-start.15 = (bf16[448,256]{1,0:T(8,128)(2,1)}, bf16[448,256]{1,0:T(8,128)(2,1)S(1)}, u32[]{:S(2)}, u32[]{:S(2)}) collective-permute-start(bf16[448,256]{1,0:T(8,128)(2,1)} %get-tuple-element.139.rest_0_), channel_id=1, source_target_pairs={{0,1},{1,0},{2,3},{3,2},{4,5},{5,4},{6,7},{7,6},{8,9},{9,8},{10,11... | collective-permute-start | bytes 688136 | tf_op jit(solution)/shard_map/ppermute | solution.py:74
  133.9 1.5 collective-permute-start.17
  135.4 6.9 %collective-permute-done.15.rest_1_ = bf16[448,256]{1,0:T(8,128)(2,1)S(1)} collective-permute-done((bf16[448,256]{1,0:T(8,128)(2,1)}, bf16[448,256]{1,0:T(8,128)(2,1)S(1)}, u32[]{:S(2)}, u32[]{:S(2)}) %collective-permute-start.15) | collective-permute-done | bytes 229408 | tf_op jit(solution)/shard_map/ppermute | solution.py:74
  142.3 10.1 %collective-permute-done.16.rest_2_ = bf16[448,256]{1,0:T(8,128)(2,1)S(1)} collective-permute-done((bf16[448,256]{1,0:T(8,128)(2,1)}, bf16[448,256]{1,0:T(8,128)(2,1)S(1)}, u32[]{:S(2)}, u32[]{:S(2)}) %collective-permute-start.16) | collective-permute-done | bytes 229408 | tf_op jit(solution)/shard_map/ppermute | solution.py:74
  153.2 13.3 %back.1 = (f32[448,256]{1,0:T(8,128)}, bf16[1792,256]{1,0:T(8,128)(2,1)}, bf16[1,256,1536]{2,1,0:T(8,128)(2,1)}, f32[8,448]{1,0:T(8,128)}, f32[448,256]{1,0:T(8,...) custom-call(s32[1]{0:T(128)} %bitcast.1.own_ref, ...), custom_call_target="tpu_custom_call" | custom-call | flops 1644167168 | bytes 16056320 | tf_op jit(solution)/shard_map/back/pallas_call | solution.py:692
  166.5 2.4 collective-permute-start.20
  168.9 2.7 collective-permute-start.19
  173.3 1.5 collective-permute-start.31
  177.9 10.9 %collective-permute-done.19 = bf16[464,256]{1,0:T(8,128)(2,1)} collective-permute-done((bf16[464,256]{1,0:T(8,128)(2,1)}, bf16[464,256]{1,0:T(8,128)(2,1)}, u32[]{:S(2)}, u32[]{:S(2)}) %collective-permute-start.19) | collective-permute-done | bytes 237600 | tf_op jit(solution)/shard_map/ppermute | solution.py:74
  189.5 2.5 fusion.7
  194.5 1.5 collective-permute-start.22
  196.0 4.5 %feed.1 = (f32[448,256]{1,0:T(8,128)}, bf16[448,256]{1,0:T(8,128)(2,1)}, bf16[448,256]{1,0:T(8,128)(2,1)}, bf16[448,256]{1,0:T(8,128)(2,1)}) custom-call(s32[1]{0:T(128)} %bitcast.1.own_ref, bf16[3,256,1024]{2,1,0:T(8,128)(2,1)} %get-tuple-element.118.act_ref.refs_5_, bf16[1024,1792]{1,0:T(8,128)(2,1)} %down_ref.3), custom_call_target="tpu_custom_call" | custom-call | flops 939524096 | bytes 3670016 | tf_op jit(solution)/shard_map/feed/pallas_call | solution.py:676
  200.4 3.4 %collective-permute-done.22 = f32[8,448]{1,0:T(8,128)S(1)} collective-permute-done((f32[8,448]{1,0:T(8,128)S(1)}, f32[8,448]{1,0:T(8,128)S(1)}, u32[]{:S(2)}, u32[]{:S(2)}) %collective-permute-start.22) | collective-permute-done | bytes 14368 | tf_op jit(solution)/shard_map/ppermute | solution.py:69
  203.9 2.4 collective-permute-start.8
  206.9 1.4 collective-permute-start.6
  208.9 5.9 %shard_map.467 = (bf16[2,224,1536]{2,1,0:T(8,128)(2,1)}, bf16[2,224,1536]{2,1,0:T(8,128)(2,1)}) custom-call(s32[3]{0:T(128)} %pad_add_fusion.2.refs_0_, bf16[4,2,224,256]{3,2,1,0:T(8,128)(2,1)} %bitcast.134, bf16[4,2,224,256]{3,2,1,0:T(8,128)(2,1)} %bitcast.18.refs_2_, bf16[4,2,224,256]{3,2,1,0:T(8,128)(2,1)} %bitcast.126, ...), custom_call_target="tpu_custom_call" | custom-call | flops 1409286144 | bytes 5505024 | tf_op jit(solution)/shard_map/pallas_call | solution.py:397
  214.8 4.2 %shard_map.465 = (bf16[2,224,768]{2,1,0:T(8,128)(2,1)}, bf16[2,224,768]{2,1,0:T(8,128)(2,1)}) custom-call(s32[3]{0:T(128)} %pad_add_fusion.refs_0_, bf16[4,2,224,256]{3,2,1,0:T(8,128)(2,1)} %bitcast.131, bf16[4,2,224,256]{3,2,1,0:T(8,128)(2,1)} %bitcast.32.refs_2_, bf16[4,2,224,256]{3,2,1,0:T(8,128)(2,1)} %bitcast.135, bf16[4,2,224,256]{3,2,1,0:T(8,128)(2,1)} %bitcast.137, ...), custom_call_target="tpu_custom_call" | custom-call | flops 704643072 | bytes 2752512 | tf_op jit(solution)/shard_map/pallas_call | solution.py:397
  219.0 1.5 collective-permute-start.23
  221.8 4.8 %shard_map.468 = (bf16[1,224,1536]{2,1,0:T(8,128)(2,1)}, bf16[1,224,1536]{2,1,0:T(8,128)(2,1)}, bf16[1,224,1536]{2,1,0:T(8,128)(2,1)}, bf16[1,224,1536]{2,1,0:T(8,128)(2,1)}) custom-call(s32[4]{0:T(128)} %pad_add_fusion.1.refs_0_, bf16[1,2,1,224,1536]{4,3,2,1,0:T(8,128)(2,1)} %bitcast.147, bf16[1,2,1,224,1536]{4,3,2,1,0:T(8,128)(2,1)} %bitcast.52.refs_2_, ...), custom_call_target="tpu_custom_call" | custom-call | flops 8257536 | bytes 8257536 | tf_op jit(solution)/shard_map/pallas_call | solution.py:434
  228.9 2.1 fusion.12
  231.0 1.5 collective-permute-start.33
  233.7 4.2 %shard_map.464 = (bf16[2,224,768]{2,1,0:T(8,128)(2,1)}, bf16[2,224,768]{2,1,0:T(8,128)(2,1)}) custom-call(s32[3]{0:T(128)} %pad_add_fusion.2.refs_0_, bf16[4,2,224,256]{3,2,1,0:T(8,128)(2,1)} %bitcast.132, bf16[4,2,224,256]{3,2,1,0:T(8,128)(2,1)} %bitcast.32.refs_2_, bf16[4,2,224,256]{3,2,1,0:T(8,128)(2,1)} %bitcast.136, bf16[4,2,224,256]{3,2,1,0:T(8,128)(2,1)} %bitcast.138, ...), custom_call_target="tpu_custom_call" | custom-call | flops 704643072 | bytes 2752512 | tf_op jit(solution)/shard_map/pallas_call | solution.py:397
  239.2 6.2 %collective-permute-done.28 = bf16[2,224,768]{2,1,0:T(8,128)(2,1)} collective-permute-done((bf16[2,224,768]{2,1,0:T(8,128)(2,1)}, bf16[2,224,768]{2,1,0:T(8,128)(2,1)}, u32[]{:S(2)}, u32[]{:S(2)}) %collective-permute-start.28) | collective-permute-done | bytes 688160 | tf_op jit(solution)/shard_map/ppermute | solution.py:69
  245.4 3.1 %shard_map.466 = (bf16[1,224,768]{2,1,0:T(8,128)(2,1)}, bf16[1,224,768]{2,1,0:T(8,128)(2,1)}, bf16[1,224,768]{2,1,0:T(8,128)(2,1)}, bf16[1,224,768]{2,1,0:T(8,128)(2,1)}) custom-call(s32[4]{0:T(128)} %pad_add_fusion.1.refs_0_, bf16[1,2,1,224,768]{4,3,2,1,0:T(8,128)(2,1)} %bitcast.149, bf16[1,2,1,224,768]{4,3,2,1,0:T(8,128)(2,1)} %bitcast.36.refs_2_, ...), custom_call_target="tpu_custom_call" | custom-call | flops 4128768 | bytes 4128768 | tf_op jit(solution)/shard_map/pallas_call | solution.py:434
  249.7 2.9 %collective-permute-done.34 = bf16[1,224,1536]{2,1,0:T(8,128)(2,1)S(1)} collective-permute-done((bf16[1,224,1536]{2,1,0:T(8,128)(2,1)}, bf16[1,224,1536]{2,1,0:T(8,128)(2,1)S(1)}, u32[]{:S(2)}, u32[]{:S(2)}) %collective-permute-start.34) | collective-permute-done | bytes 688160 | tf_op jit(solution)/shard_map/ppermute | solution.py:69
  252.8 5.8 %collective-permute-done.33 = bf16[1,224,1536]{2,1,0:T(8,128)(2,1)} collective-permute-done((bf16[1,224,1536]{2,1,0:T(8,128)(2,1)}, bf16[1,224,1536]{2,1,0:T(8,128)(2,1)}, u32[]{:S(2)}, u32[]{:S(2)}) %collective-permute-start.33) | collective-permute-done | bytes 688160 | tf_op jit(solution)/shard_map/ppermute | solution.py:69
  258.6 6.0 %adv.1 = (f32[3584,128]{1,0:T(8,128)}, f32[3584,128]{1,0:T(8,128)}, f32[3584,128]{1,0:T(8,128)}, f32[3584,128]{1,0:T(8,128)}) custom-call(bf16[224,1536]{1,0:T(8,128)(2,1)} %bitcast.151, bf16[224,1536]{1,0:T(8,128)(2,1)} %bitcast.56.refs_1_, bf16[224,1536]{1,0:T(8,128)(2,1)} %bitcast.141, bf16[224,1536]{1,0:T(8,128)(2,1)} %bitcast.144, ...), custom_call_target="tpu_custom_call" | custom-call | flops 2293760 | bytes 14680064 | tf_op jit(solution)/shard_map/adv/pallas_call | solution.py:487
  264.6 3.3 %multiply_add_fusion = (f32[1024,224]{0,1:T(8,128)}, f32[1024,224]{0,1:T(8,128)}, f32[1024,224]{0,1:T(8,128)}) fusion(f32[1024,224]{0,1:T(8,128)} %param.47, f32[1024,224]{0,1:T(8,128)S(1)} %convert_element_type.103, f32[1024,224]{0,1:T(8,128)S(1)} %add_bitcast_fusion, f32[1024,224]{0,1:T(8,128)} %param.40), kind=kLoop, calls=%fused_computation.1 | loop fusion | flops 2293760 | bytes 6422528 | tf_op jit(solution)/shard_map/add | solution.py:33
  267.9 7.2 %last.1 = (f32[224,2,448]{2,1,0:T(2,128)}, f32[224,2,448]{2,1,0:T(2,128)}, f32[224,2,448]{2,1,0:T(2,128)}, f32[224,2,448]{2,1,0:T(2,128)}, f32[128,224]{1,0:T(8,...) custom-call(bf16[224,768]{1,0:T(8,128)(2,1)} %bitcast.153, ...), custom_call_target="tpu_custom_call" | custom-call | flops 3010560 | bytes 10035200 | tf_op jit(solution)/shard_map/last/pallas_call | solution.py:767
  (139 shorter events, 29.5 us)
Async XLA Ops:
  0.7 29.6 %copy-start.27 = (s32[256]{0:T(256)S(1)}, s32[256]{0:T(256)}, u32[]{:S(2)}) copy-start(s32[256]{0:T(256)} %param.26) | copy-start | bytes 3076
  3.3 59.8 %copy-start.13 = (bf16[448,256]{1,0:T(8,128)(2,1)}, bf16[448,256]{1,0:T(8,128)(2,1)S(1)}, u32[]{:S(2)}) copy-start(bf16[448,256]{1,0:T(8,128)(2,1)S(1)} %select_bitcast_fusion.rest_0_) | copy-start | bytes 688132
  28.0 60.6 %collective-permute-start.3 = (bf16[448,256]{1,0:T(8,128)(2,1)S(1)}, bf16[448,256]{1,0:T(8,128)(2,1)S(1)}, u32[]{:S(2)}, u32[]{:S(2)}) collective-permute-start(bf16[448,256]{1,0:T(8,128)(2,1)S(1)} %select_bitcast_fusion.rest_0_), channel_id=1, source_target_pairs={{0,1},{1,0},{2,3},{3,2},{4,5},{5,4},{6,7},{7,6},{8,9},{9,8},{10,11... | collective-permute-start | bytes 688136 | tf_op jit(solution)/shard_map/ppermute | solution.py:74
  28.0 60.7 %collective-permute-start.4 = (bf16[448,256]{1,0:T(8,128)(2,1)S(1)}, bf16[448,256]{1,0:T(8,128)(2,1)S(1)}, u32[]{:S(2)}, u32[]{:S(2)}) collective-permute-start(bf16[448,256]{1,0:T(8,128)(2,1)S(1)} %select_bitcast_fusion.rest_0_), channel_id=1, source_target_pairs={{0,2},{1,3},{2,0},{3,1},{4,6},{5,7},{6,4},{7,5},{8,10},{9,11},{10,... | collective-permute-start | bytes 688136 | tf_op jit(solution)/shard_map/ppermute | solution.py:74
  38.9 24.3 %collective-permute-start.2 = (bf16[448,256]{1,0:T(8,128)(2,1)}, bf16[448,256]{1,0:T(8,128)(2,1)S(1)}, u32[]{:S(2)}, u32[]{:S(2)}) collective-permute-start(bf16[448,256]{1,0:T(8,128)(2,1)} %get-tuple-element.115), channel_id=1, source_target_pairs={{0,3},{1,2},{2,1},{3,0},{4,7},{5,6},{6,5},{7,4},{8,11},{9,10},{10,... | collective-permute-start | bytes 688136 | tf_op jit(solution)/shard_map/ppermute | solution.py:74
  41.0 24.3 %collective-permute-start.1 = (bf16[448,256]{1,0:T(8,128)(2,1)}, bf16[448,256]{1,0:T(8,128)(2,1)S(1)}, u32[]{:S(2)}, u32[]{:S(2)}) collective-permute-start(bf16[448,256]{1,0:T(8,128)(2,1)} %get-tuple-element.114), channel_id=1, source_target_pairs={{0,2},{1,3},{2,0},{3,1},{4,6},{5,7},{6,4},{7,5},{8,10},{9,11},{10,... | collective-permute-start | bytes 688136 | tf_op jit(solution)/shard_map/ppermute | solution.py:74
  41.0 24.3 %collective-permute-start = (bf16[448,256]{1,0:T(8,128)(2,1)}, bf16[448,256]{1,0:T(8,128)(2,1)S(1)}, u32[]{:S(2)}, u32[]{:S(2)}) collective-permute-start(bf16[448,256]{1,0:T(8,128)(2,1)} %get-tuple-element.113), channel_id=1, source_target_pairs={{0,1},{1,0},{2,3},{3,2},{4,5},{5,4},{6,7},{7,6},{8,9},{9,8},{10,11... | collective-permute-start | bytes 688136 | tf_op jit(solution)/shard_map/ppermute | solution.py:74
  63.1 25.5 %collective-permute-start.5 = (bf16[448,256]{1,0:T(8,128)(2,1)S(1)}, bf16[448,256]{1,0:T(8,128)(2,1)S(1)}, u32[]{:S(2)}, u32[]{:S(2)}) collective-permute-start(bf16[448,256]{1,0:T(8,128)(2,1)S(1)} %select_bitcast_fusion.rest_0_), channel_id=1, source_target_pairs={{0,3},{1,2},{2,1},{3,0},{4,7},{5,6},{6,5},{7,4},{8,11},{9,10},{10,... | collective-permute-start | bytes 688136 | tf_op jit(solution)/shard_map/ppermute | solution.py:74
  65.3 38.5 %copy-start.9 = (bf16[448,256]{1,0:T(8,128)(2,1)}, bf16[448,256]{1,0:T(8,128)(2,1)S(1)}, u32[]{:S(2)}) copy-start(bf16[448,256]{1,0:T(8,128)(2,1)S(1)} %collective-permute-done) | copy-start | bytes 688132
  103.8 9.9 %collective-permute-start.14 = (bf16[3,256,1024]{2,1,0:T(8,128)(2,1)}, bf16[3,256,1024]{2,1,0:T(8,128)(2,1)S(1)}, u32[]{:S(2)}, u32[]{:S(2)}) collective-permute-start(bf16[3,256,1024]{2,1,0:T(8,128)(2,1)} %get-tuple-element.118.act_ref.refs_5_), channel_id=1, source_target_pairs={{0,4},{4,0},{8,12},{12,8},{16,20},{20,16},{24,28},{28,24},{1,5},{5... | collective-permute-start | bytes 4718600 | tf_op jit(solution)/shard_map/ppermute | solution.py:69
  103.8 5.3 %collective-permute-start.12 = (bf16[1792,256]{1,0:T(8,128)(2,1)}, bf16[1792,256]{1,0:T(8,128)(2,1)}, u32[]{:S(2)}, u32[]{:S(2)}) collective-permute-start(bf16[1792,256]{1,0:T(8,128)(2,1)} %get-tuple-element.136), channel_id=1, source_target_pairs={{0,4},{4,0},{8,12},{12,8},{16,20},{20,16},{24,28},{28,24},{1,5},{5... | collective-permute-start | bytes 2752520 | tf_op jit(solution)/shard_map/ppermute | solution.py:69
  104.3 9.4 %collective-permute-start.13 = (bf16[1792,256]{1,0:T(8,128)(2,1)}, bf16[1792,256]{1,0:T(8,128)(2,1)}, u32[]{:S(2)}, u32[]{:S(2)}) collective-permute-start(bf16[1792,256]{1,0:T(8,128)(2,1)} %get-tuple-element.124.cot_ref), channel_id=1, source_target_pairs={{0,4},{4,0},{8,12},{12,8},{16,20},{20,16},{24,28},{28,24},{1,5},{5... | collective-permute-start | bytes 2752520 | tf_op jit(solution)/shard_map/ppermute | solution.py:69
  104.4 16.1 %collective-permute-start.9 = (bf16[448,256]{1,0:T(8,128)(2,1)}, bf16[448,256]{1,0:T(8,128)(2,1)S(1)}, u32[]{:S(2)}, u32[]{:S(2)}) collective-permute-start(bf16[448,256]{1,0:T(8,128)(2,1)} %get-tuple-element.133), channel_id=1, source_target_pairs={{0,1},{1,0},{2,3},{3,2},{4,5},{5,4},{6,7},{7,6},{8,9},{9,8},{10,11... | collective-permute-start | bytes 688136 | tf_op jit(solution)/shard_map/ppermute | solution.py:74
  106.5 19.6 %collective-permute-start.10 = (bf16[448,256]{1,0:T(8,128)(2,1)}, bf16[448,256]{1,0:T(8,128)(2,1)}, u32[]{:S(2)}, u32[]{:S(2)}) collective-permute-start(bf16[448,256]{1,0:T(8,128)(2,1)} %get-tuple-element.134), channel_id=1, source_target_pairs={{0,2},{1,3},{2,0},{3,1},{4,6},{5,7},{6,4},{7,5},{8,10},{9,11},{10,... | collective-permute-start | bytes 688136 | tf_op jit(solution)/shard_map/ppermute | solution.py:74
  109.1 16.9 %collective-permute-start.11 = (bf16[448,256]{1,0:T(8,128)(2,1)}, bf16[448,256]{1,0:T(8,128)(2,1)}, u32[]{:S(2)}, u32[]{:S(2)}) collective-permute-start(bf16[448,256]{1,0:T(8,128)(2,1)} %get-tuple-element.135), channel_id=1, source_target_pairs={{0,3},{1,2},{2,1},{3,0},{4,7},{5,6},{6,5},{7,4},{8,11},{9,10},{10,... | collective-permute-start | bytes 688136 | tf_op jit(solution)/shard_map/ppermute | solution.py:74
  126.0 9.4 %copy-start.3 = (bf16[1792,256]{1,0:T(8,128)(2,1)S(1)}, bf16[1792,256]{1,0:T(8,128)(2,1)}, u32[]{:S(2)}) copy-start(bf16[1792,256]{1,0:T(8,128)(2,1)} %get-tuple-element.148) | copy-start | bytes 2752516
  128.3 14.0 %collective-permute-start.15 = (bf16[448,256]{1,0:T(8,128)(2,1)}, bf16[448,256]{1,0:T(8,128)(2,1)S(1)}, u32[]{:S(2)}, u32[]{:S(2)}) collective-permute-start(bf16[448,256]{1,0:T(8,128)(2,1)} %get-tuple-element.139.rest_0_), channel_id=1, source_target_pairs={{0,1},{1,0},{2,3},{3,2},{4,5},{5,4},{6,7},{7,6},{8,9},{9,8},{10,11... | collective-permute-start | bytes 688136 | tf_op jit(solution)/shard_map/ppermute | solution.py:74
  133.0 19.4 %collective-permute-start.16 = (bf16[448,256]{1,0:T(8,128)(2,1)}, bf16[448,256]{1,0:T(8,128)(2,1)S(1)}, u32[]{:S(2)}, u32[]{:S(2)}) collective-permute-start(bf16[448,256]{1,0:T(8,128)(2,1)} %get-tuple-element.139.rest_0_), channel_id=1, source_target_pairs={{0,2},{1,3},{2,0},{3,1},{4,6},{5,7},{6,4},{7,5},{8,10},{9,11},{10,... | collective-permute-start | bytes 688136 | tf_op jit(solution)/shard_map/ppermute | solution.py:74
  133.9 18.5 %collective-permute-start.17 = (bf16[448,256]{1,0:T(8,128)(2,1)}, bf16[448,256]{1,0:T(8,128)(2,1)S(1)}, u32[]{:S(2)}, u32[]{:S(2)}) collective-permute-start(bf16[448,256]{1,0:T(8,128)(2,1)} %get-tuple-element.139.rest_0_), channel_id=1, source_target_pairs={{0,3},{1,2},{2,1},{3,0},{4,7},{5,6},{6,5},{7,4},{8,11},{9,10},{10,... | collective-permute-start | bytes 688136 | tf_op jit(solution)/shard_map/ppermute | solution.py:74
  135.4 59.1 %collective-permute-start.24 = (bf16[1792,256]{1,0:T(8,128)(2,1)S(1)}, bf16[1792,256]{1,0:T(8,128)(2,1)}, u32[]{:S(2)}, u32[]{:S(2)}) collective-permute-start(bf16[1792,256]{1,0:T(8,128)(2,1)S(1)} %copy-done.3), channel_id=1, source_target_pairs={{0,4},{4,0},{8,12},{12,8},{16,20},{20,16},{24,28},{28,24},{1,5},{5... | collective-permute-start | bytes 2752520 | tf_op jit(solution)/shard_map/ppermute | solution.py:69
  142.3 10.9 %copy-start.16 = (bf16[448,256]{1,0:T(8,128)(2,1)}, bf16[448,256]{1,0:T(8,128)(2,1)S(1)}, u32[]{:S(2)}) copy-start(bf16[448,256]{1,0:T(8,128)(2,1)S(1)} %collective-permute-done.15.rest_1_) | copy-start | bytes 688132
  153.2 18.6 %copy-start.22 = (bf16[2,448]{1,0:T(2,128)(2,1)S(1)}, bf16[2,448]{1,0:T(2,128)(2,1)}, u32[]{:S(2)}) copy-start(bf16[2,448]{1,0:T(2,128)(2,1)} %param.27) | copy-start | bytes 5380
  153.2 21.6 %copy-start.11 = (f32[448,256]{1,0:T(8,128)S(1)}, f32[448,256]{1,0:T(8,128)}, u32[]{:S(2)}) copy-start(f32[448,256]{1,0:T(8,128)} %get-tuple-element.146) | copy-start | bytes 1376260
  166.5 10.1 %collective-permute-start.20 = (bf16[464,256]{1,0:T(8,128)(2,1)}, bf16[464,256]{1,0:T(8,128)(2,1)S(1)}, u32[]{:S(2)}, u32[]{:S(2)}) collective-permute-start(bf16[464,256]{1,0:T(8,128)(2,1)} %get-tuple-element.144), channel_id=1, source_target_pairs={{0,3},{1,2},{2,1},{3,0},{4,7},{5,6},{6,5},{7,4},{8,11},{9,10},{10,... | collective-permute-start | bytes 712712 | tf_op jit(solution)/shard_map/ppermute | solution.py:74
  168.9 19.8 %collective-permute-start.19 = (bf16[464,256]{1,0:T(8,128)(2,1)}, bf16[464,256]{1,0:T(8,128)(2,1)}, u32[]{:S(2)}, u32[]{:S(2)}) collective-permute-start(bf16[464,256]{1,0:T(8,128)(2,1)} %get-tuple-element.143), channel_id=1, source_target_pairs={{0,2},{1,3},{2,0},{3,1},{4,6},{5,7},{6,4},{7,5},{8,10},{9,11},{10,... | collective-permute-start | bytes 712712 | tf_op jit(solution)/shard_map/ppermute | solution.py:74
  171.6 17.2 %collective-permute-start.18 = (bf16[464,256]{1,0:T(8,128)(2,1)}, bf16[464,256]{1,0:T(8,128)(2,1)}, u32[]{:S(2)}, u32[]{:S(2)}) collective-permute-start(bf16[464,256]{1,0:T(8,128)(2,1)} %get-tuple-element.142), channel_id=1, source_target_pairs={{0,1},{1,0},{2,3},{3,2},{4,5},{5,4},{6,7},{7,6},{8,9},{9,8},{10,11... | collective-permute-start | bytes 712712 | tf_op jit(solution)/shard_map/ppermute | solution.py:74
  173.3 45.7 %collective-permute-start.31 = (bf16[2,224,1536]{2,1,0:T(8,128)(2,1)}, bf16[2,224,1536]{2,1,0:T(8,128)(2,1)}, u32[]{:S(2)}, u32[]{:S(2)}) collective-permute-start(bf16[2,224,1536]{2,1,0:T(8,128)(2,1)} %get-tuple-element.137.refs_4_), channel_id=1, source_target_pairs={{0,8},{4,12},{8,0},{12,4},{16,24},{20,28},{24,16},{28,20},{1,9},{5... | collective-permute-start | bytes 4128776 | tf_op jit(solution)/shard_map/ppermute | solution.py:69
  176.6 12.1 %copy-start.20 = (bf16[464,256]{1,0:T(8,128)(2,1)}, bf16[464,256]{1,0:T(8,128)(2,1)S(1)}, u32[]{:S(2)}) copy-start(bf16[464,256]{1,0:T(8,128)(2,1)S(1)} %collective-permute-done.20) | copy-start | bytes 712708
  176.6 43.9 %collective-permute-start.32 = (bf16[2,224,1536]{2,1,0:T(8,128)(2,1)}, bf16[2,224,1536]{2,1,0:T(8,128)(2,1)}, u32[]{:S(2)}, u32[]{:S(2)}) collective-permute-start(bf16[2,224,1536]{2,1,0:T(8,128)(2,1)} %get-tuple-element.138.refs_5_), channel_id=1, source_target_pairs={{0,16},{4,20},{8,24},{12,28},{16,0},{20,4},{24,8},{28,12},{1,17},{... | collective-permute-start | bytes 4128776 | tf_op jit(solution)/shard_map/ppermute | solution.py:69
  188.7 18.2 %collective-permute-start.25 = (bf16[1792,256]{1,0:T(8,128)(2,1)}, bf16[1792,256]{1,0:T(8,128)(2,1)S(1)}, u32[]{:S(2)}, u32[]{:S(2)}) collective-permute-start(bf16[1792,256]{1,0:T(8,128)(2,1)} %get-tuple-element.149), channel_id=1, source_target_pairs={{0,4},{4,0},{8,12},{12,8},{16,20},{20,16},{24,28},{28,24},{1,5},{5... | collective-permute-start | bytes 2752520 | tf_op jit(solution)/shard_map/ppermute | solution.py:69
  192.1 1.4 collective-permute-start.21
  193.5 12.8 %collective-permute-start.26 = (bf16[1,256,1536]{2,1,0:T(8,128)(2,1)}, bf16[1,256,1536]{2,1,0:T(8,128)(2,1)}, u32[]{:S(2)}, u32[]{:S(2)}) collective-permute-start(bf16[1,256,1536]{2,1,0:T(8,128)(2,1)} %get-tuple-element.150.refs_5_), channel_id=1, source_target_pairs={{0,4},{4,0},{8,12},{12,8},{16,20},{20,16},{24,28},{28,24},{1,5},{5... | collective-permute-start | bytes 2359304 | tf_op jit(solution)/shard_map/ppermute | solution.py:69
  194.5 9.4 %collective-permute-start.22 = (f32[8,448]{1,0:T(8,128)S(1)}, f32[8,448]{1,0:T(8,128)S(1)}, u32[]{:S(2)}, u32[]{:S(2)}) collective-permute-start(f32[8,448]{1,0:T(8,128)S(1)} %fusion.23), channel_id=1, source_target_pairs={{0,8},{4,12},{8,0},{12,4},{16,24},{20,28},{24,16},{28,20},{1,9},{5... | collective-permute-start | bytes 43016 | tf_op jit(solution)/shard_map/ppermute | solution.py:69
  203.9 22.8 %collective-permute-start.8 = (bf16[448,256]{1,0:T(8,128)(2,1)}, bf16[448,256]{1,0:T(8,128)(2,1)S(1)}, u32[]{:S(2)}, u32[]{:S(2)}) collective-permute-start(bf16[448,256]{1,0:T(8,128)(2,1)} %get-tuple-element.122), channel_id=1, source_target_pairs={{0,3},{1,2},{2,1},{3,0},{4,7},{5,6},{6,5},{7,4},{8,11},{9,10},{10,... | collective-permute-start | bytes 688136 | tf_op jit(solution)/shard_map/ppermute | solution.py:74
  206.3 21.2 %collective-permute-start.7 = (bf16[448,256]{1,0:T(8,128)(2,1)}, bf16[448,256]{1,0:T(8,128)(2,1)S(1)}, u32[]{:S(2)}, u32[]{:S(2)}) collective-permute-start(bf16[448,256]{1,0:T(8,128)(2,1)} %get-tuple-element.121), channel_id=1, source_target_pairs={{0,2},{1,3},{2,0},{3,1},{4,6},{5,7},{6,4},{7,5},{8,10},{9,11},{10,... | collective-permute-start | bytes 688136 | tf_op jit(solution)/shard_map/ppermute | solution.py:74
  206.9 7.9 %copy-start.4 = (bf16[1792,256]{1,0:T(8,128)(2,1)}, bf16[1792,256]{1,0:T(8,128)(2,1)S(1)}, u32[]{:S(2)}) copy-start(bf16[1792,256]{1,0:T(8,128)(2,1)S(1)} %collective-permute-done.25) | copy-start | bytes 2752516
  206.9 21.9 %collective-permute-start.6 = (bf16[448,256]{1,0:T(8,128)(2,1)}, bf16[448,256]{1,0:T(8,128)(2,1)}, u32[]{:S(2)}, u32[]{:S(2)}) collective-permute-start(bf16[448,256]{1,0:T(8,128)(2,1)} %get-tuple-element.120), channel_id=1, source_target_pairs={{0,1},{1,0},{2,3},{3,2},{4,5},{5,4},{6,7},{7,6},{8,9},{9,8},{10,11... | collective-permute-start | bytes 688136 | tf_op jit(solution)/shard_map/ppermute | solution.py:74
  219.0 11.9 %collective-permute-start.23 = (f32[8,448]{1,0:T(8,128)S(1)}, f32[8,448]{1,0:T(8,128)S(1)}, u32[]{:S(2)}, u32[]{:S(2)}) collective-permute-start(f32[8,448]{1,0:T(8,128)S(1)} %add.146), channel_id=1, source_target_pairs={{0,16},{4,20},{8,24},{12,28},{16,0},{20,4},{24,8},{28,12},{1,17},{... | collective-permute-start | bytes 43016 | tf_op jit(solution)/shard_map/ppermute | solution.py:69
  220.6 18.6 %collective-permute-start.27 = (bf16[2,224,768]{2,1,0:T(8,128)(2,1)}, bf16[2,224,768]{2,1,0:T(8,128)(2,1)}, u32[]{:S(2)}, u32[]{:S(2)}) collective-permute-start(bf16[2,224,768]{2,1,0:T(8,128)(2,1)} %get-tuple-element.152), channel_id=1, source_target_pairs={{0,8},{4,12},{8,0},{12,4},{16,24},{20,28},{24,16},{28,20},{1,9},{5... | collective-permute-start | bytes 2064392 | tf_op jit(solution)/shard_map/ppermute | solution.py:69
  221.8 7.0 %copy-start.10 = (bf16[448,256]{1,0:T(8,128)(2,1)S(1)}, bf16[448,256]{1,0:T(8,128)(2,1)}, u32[]{:S(2)}) copy-start(bf16[448,256]{1,0:T(8,128)(2,1)} %copy-done.9) | copy-start | bytes 688132
  221.8 7.1 %copy-start.12 = (f32[448,256]{1,0:T(8,128)S(1)}, f32[448,256]{1,0:T(8,128)}, u32[]{:S(2)}) copy-start(f32[448,256]{1,0:T(8,128)} %get-tuple-element.119) | copy-start | bytes 1376260
  226.7 18.7 %collective-permute-start.28 = (bf16[2,224,768]{2,1,0:T(8,128)(2,1)}, bf16[2,224,768]{2,1,0:T(8,128)(2,1)}, u32[]{:S(2)}, u32[]{:S(2)}) collective-permute-start(bf16[2,224,768]{2,1,0:T(8,128)(2,1)} %get-tuple-element.154), channel_id=1, source_target_pairs={{0,16},{4,20},{8,24},{12,28},{16,0},{20,4},{24,8},{28,12},{1,17},{... | collective-permute-start | bytes 2064392 | tf_op jit(solution)/shard_map/ppermute | solution.py:69
  228.2 24.4 %collective-permute-start.34 = (bf16[1,224,1536]{2,1,0:T(8,128)(2,1)}, bf16[1,224,1536]{2,1,0:T(8,128)(2,1)S(1)}, u32[]{:S(2)}, u32[]{:S(2)}) collective-permute-start(bf16[1,224,1536]{2,1,0:T(8,128)(2,1)} %get-tuple-element.170), channel_id=1, source_target_pairs={{0,8},{4,12},{8,0},{12,4},{16,24},{20,28},{24,16},{28,20},{1,9},{5... | collective-permute-start | bytes 2064392 | tf_op jit(solution)/shard_map/ppermute | solution.py:69
  231.0 27.6 %collective-permute-start.33 = (bf16[1,224,1536]{2,1,0:T(8,128)(2,1)}, bf16[1,224,1536]{2,1,0:T(8,128)(2,1)}, u32[]{:S(2)}, u32[]{:S(2)}) collective-permute-start(bf16[1,224,1536]{2,1,0:T(8,128)(2,1)} %get-tuple-element.168), channel_id=1, source_target_pairs={{0,16},{4,20},{8,24},{12,28},{16,0},{20,4},{24,8},{28,12},{1,17},{... | collective-permute-start | bytes 2064392 | tf_op jit(solution)/shard_map/ppermute | solution.py:69
  237.9 14.7 %copy-start.5 = (bf16[1,224,1536]{2,1,0:T(8,128)(2,1)S(1)}, bf16[1,224,1536]{2,1,0:T(8,128)(2,1)}, u32[]{:S(2)}) copy-start(bf16[1,224,1536]{2,1,0:T(8,128)(2,1)} %get-tuple-element.169) | copy-start | bytes 2064388
  248.4 19.5 %collective-permute-start.29 = (bf16[1,224,768]{2,1,0:T(8,128)(2,1)}, bf16[1,224,768]{2,1,0:T(8,128)(2,1)}, u32[]{:S(2)}, u32[]{:S(2)}) collective-permute-start(bf16[1,224,768]{2,1,0:T(8,128)(2,1)} %get-tuple-element.156), channel_id=1, source_target_pairs={{0,16},{4,20},{8,24},{12,28},{16,0},{20,4},{24,8},{28,12},{1,17},{... | collective-permute-start | bytes 1032200 | tf_op jit(solution)/shard_map/ppermute | solution.py:69
  249.2 18.7 %collective-permute-start.30 = (bf16[1,224,768]{2,1,0:T(8,128)(2,1)}, bf16[1,224,768]{2,1,0:T(8,128)(2,1)}, u32[]{:S(2)}, u32[]{:S(2)}) collective-permute-start(bf16[1,224,768]{2,1,0:T(8,128)(2,1)} %get-tuple-element.158), channel_id=1, source_target_pairs={{0,8},{4,12},{8,0},{12,4},{16,24},{20,28},{24,16},{28,20},{1,9},{5... | collective-permute-start | bytes 1032200 | tf_op jit(solution)/shard_map/ppermute | solution.py:69
  252.7 11.8 %copy-start.1 = (f32[1024,224]{0,1:T(8,128)}, f32[1024,224]{0,1:T(8,128)S(1)}, u32[]{:S(2)}) copy-start(f32[1024,224]{0,1:T(8,128)S(1)} %add_bitcast_fusion) | copy-start | bytes 2752516
  (18 other events, 69.9 us)
